TPU v7x, 128 devices: a whole 4x4x4 slice. The times are simulated.
128 devices in a mesh: segment: 4 (over y), dp: 32 (over z, x, core).
Axes of the slice: x: 4, y: 4, z: 4, core: 2. Of those that a mesh axis runs over, the one named last changes fastest.
Arguments:
- video_clips: bfloat16 [32, 9, 192, 128], P('dp'), may hold values from -6 to 6
- conv_weight: bfloat16 [4, 192, 5184], P('segment'), may hold values from -0.078125 to 0.078125
- norm_gain: float32 [4, 192], P('segment'), may hold values from 0.1 to 1.9
- cotangent: bfloat16 [32, 9, 192, 128], P('dp'), may hold values from -12 to 12
- clip_groups: int32 [32], P('dp'), may hold values from 1 to 3, as said below
Outputs:
- section_features: bfloat16 [4, 32, 9, 192, 128], P('segment', 'dp')
- grad_weight: float32 [4, 192, 5184], P('segment', 'dp')
- grad_gain: float32 [4, 192], P('segment', 'dp')
Inputs may be any that keep to these rules, and one draw needn't show every extreme that they name: `clip_groups`: A clip of k groups has 4 * k - 3 frames; later frames are not part of it. Some clip has 3 groups.
All inputs are finite; a program needn't handle non-finite values.
Results may differ from a plain program's by a relative error of at most 0.0095.
Values may be sent and summed in bfloat16 or wider, within the bound.
A program may use at most 128 MiB of HBM per device.

v0:
```python
import jax
import jax.numpy as jnp
from jax import lax
from jax.sharding import PartitionSpec as P

TILE_H = 8
TILE_W = 16


epsilon = 1e-06


def shifted(block, axis, distance):
    devices = range(lax.axis_size(axis))
    route = [(i - distance, i) for i in devices if i - distance in devices]
    return lax.ppermute(block, axis, route)


def normalize(values, gain_vec):
    scale = lax.rsqrt(jnp.mean(values * values, axis=1, keepdims=True) + epsilon)
    return values * scale * gain_vec[None, :, None]


def make_patches(normed):
    frames = normed.shape[0]
    blocks = frames - 2
    channels = normed.shape[1]
    positions = normed.shape[2]
    grid = normed.reshape(frames, channels, TILE_H, TILE_W)
    padded = jnp.pad(grid, ((0, 0), (0, 0), (1, 1), (1, 1)))
    spatial = jnp.stack(
        [
            padded[:, :, row : row + TILE_H, col : col + TILE_W].reshape(
                frames, channels, positions
            )
            for row in range(3)
            for col in range(3)
        ],
        axis=1,
    )
    stacked = jnp.concatenate([spatial[tap : tap + blocks] for tap in range(3)], axis=1)
    return stacked.reshape(blocks, 27 * channels, positions)


def section_forward(window, kernel, gain_vec, frame_mask):
    normed = normalize(window.astype(jnp.float32), gain_vec).astype(jnp.bfloat16)
    patches = make_patches(normed)
    conv = jnp.einsum("ok,fkp->fop", kernel, patches, preferred_element_type=jnp.float32)
    result = (
        (window[2:].astype(jnp.float32) + jax.nn.silu(conv)) * frame_mask[:, None, None]
    ).astype(jnp.bfloat16)
    return (result, conv)


def section_backward(window, kernel, gain_vec, frame_mask, upstream, conv):
    as_float = window.astype(jnp.float32)
    normed_float, norm_back = jax.vjp(normalize, as_float, gain_vec)
    normed = normed_float.astype(jnp.bfloat16)
    patches = make_patches(normed)
    grad_z = upstream * frame_mask[:, None, None]
    sigmoid = jax.nn.sigmoid(conv)
    grad_conv = (grad_z * sigmoid * (1.0 + conv * (1.0 - sigmoid))).astype(jnp.bfloat16)
    weight_part = jnp.einsum("fop,fkp->ok", grad_conv, patches, preferred_element_type=jnp.float32)
    grad_patch = jnp.einsum("ok,fop->fkp", kernel, grad_conv, preferred_element_type=jnp.float32)
    unused, patch_back = jax.vjp(make_patches, jnp.zeros(window.shape, jnp.float32))
    grad_normed = patch_back(grad_patch)[0]
    window_grad, gain_part = norm_back(grad_normed)
    window_grad = window_grad.at[2:].add(grad_z)
    return (window_grad, weight_part, gain_part)


def body(video_clips, conv_weight, norm_gain, cotangent, clip_groups):
    num_segments = lax.axis_size("segment")
    my_segment = lax.axis_index("segment")
    frames = video_clips.shape[1]
    channels = video_clips.shape[2]
    positions = video_clips.shape[3]
    padded_len = frames + 3
    kernel = conv_weight[0]
    gain_vec = norm_gain[0]
    places = jnp.arange(padded_len, dtype=jnp.int32)
    frame_mask = ((places >= 3) & (places < 4 * clip_groups[0])).astype(jnp.float32)
    masked = video_clips[0] * frame_mask[3:, None, None].astype(jnp.bfloat16)
    source = jnp.concatenate([jnp.zeros((5, channels, positions), jnp.bfloat16), masked])
    targets = jnp.concatenate(
        [jnp.zeros((3, channels, positions), jnp.float32), cotangent[0].astype(jnp.float32)]
    )
    block_len, first_frame, num_blocks = (4, 0, padded_len // 4)
    num_turns = num_blocks + num_segments - 1

    def locate(block_index):
        usable = (block_index >= 0) & (block_index < num_blocks)
        offset = first_frame + jnp.clip(block_index, 0, num_blocks - 1) * block_len
        return (usable, offset)

    def advance(turn_index, carried):
        held_inputs, held_outputs, held_conv, incoming = carried
        usable, offset = locate(turn_index - my_segment)
        arrived = jnp.where(
            my_segment == 0, lax.dynamic_slice_in_dim(source, offset + 2, block_len), incoming
        )
        held_inputs = jnp.where(
            usable,
            lax.dynamic_update_slice_in_dim(held_inputs, arrived, offset + 2, 0),
            held_inputs,
        )
        window = lax.dynamic_slice_in_dim(held_inputs, offset, block_len + 2)
        result, conv = section_forward(
            window, kernel, gain_vec, lax.dynamic_slice_in_dim(frame_mask, offset, block_len)
        )
        held_outputs = jnp.where(
            usable, lax.dynamic_update_slice_in_dim(held_outputs, result, offset, 0), held_outputs
        )
        held_conv = jnp.where(
            usable, lax.dynamic_update_slice_in_dim(held_conv, conv, offset, 0), held_conv
        )
        incoming = shifted(result, "segment", 1)
        return (held_inputs, held_outputs, held_conv, incoming)

    forward_start = (
        jnp.zeros((padded_len + 2, channels, positions), jnp.bfloat16),
        jnp.zeros((padded_len, channels, positions), jnp.bfloat16),
        jnp.zeros((padded_len, channels, positions), jnp.float32),
        jnp.zeros((block_len, channels, positions), jnp.bfloat16),
    )
    held_inputs, held_outputs, held_conv, unused_block = lax.fori_loop(
        0, num_turns, advance, forward_start
    )

    def retreat(turn_index, carried):
        upstream, tail_grad, weight_sum, gain_sum = carried
        lateness = turn_index - (num_segments - 1 - my_segment)
        usable, offset = locate(num_blocks - 1 - lateness)
        usable = usable & (lateness >= 0) & (lateness < num_blocks)
        arrived = jnp.where(
            my_segment == num_segments - 1,
            lax.dynamic_slice_in_dim(targets, offset, block_len),
            upstream,
        )
        window = lax.dynamic_slice_in_dim(held_inputs, offset, block_len + 2)
        conv = lax.dynamic_slice_in_dim(held_conv, offset, block_len)
        window_grad, weight_part, gain_part = section_backward(
            window,
            kernel,
            gain_vec,
            lax.dynamic_slice_in_dim(frame_mask, offset, block_len),
            arrived,
            conv,
        )
        summed = window_grad + jnp.concatenate(
            [jnp.zeros((block_len, channels, positions), jnp.float32), tail_grad]
        )
        tail_grad = jnp.where(usable, summed[:2], tail_grad)
        weight_sum = jnp.where(usable, weight_sum + weight_part, weight_sum)
        gain_sum = jnp.where(usable, gain_sum + gain_part, gain_sum)
        upstream = shifted(summed[2:], "segment", -1)
        return (upstream, tail_grad, weight_sum, gain_sum)

    backward_start = (
        jnp.zeros((block_len, channels, positions), jnp.float32),
        jnp.zeros((2, channels, positions), jnp.float32),
        jnp.zeros(kernel.shape, jnp.float32),
        jnp.zeros(gain_vec.shape, jnp.float32),
    )
    finished = lax.fori_loop(0, num_turns, retreat, backward_start)
    weight_grad, gain_grad = (
        lax.psum_scatter(finished[2], "dp", scatter_dimension=0, tiled=True),
        lax.psum_scatter(finished[3], "dp", scatter_dimension=0, tiled=True),
    )
    return (held_outputs[3:][None, None], weight_grad[None], gain_grad[None])


def solution(mesh):
    placed = (
        P("dp", None, None, None),
        P("segment", None, None),
        P("segment", None),
        P("dp", None, None, None),
        P("dp"),
    )
    return jax.shard_map(
        body,
        mesh=mesh,
        in_specs=placed,
        out_specs=(
            P("segment", "dp", None, None, None),
            P("segment", "dp", None),
            P("segment", "dp"),
        ),
        check_vma=False,
    )
```

profile of v0, /device:TPU:1, one launch (start us, length us, event | category | flops | bytes accessed | tf_op | source)
XLA Modules:
  0.0 782.3 jit_solution(8760683199200884322)
XLA Ops:
  14.9 250.3 %while.44 = (s32[]{:T(128)}, bf16[14,192,128]{2,1,0:T(8,128)(2,1)S(1)}, bf16[12,192,128]{2,1,0:T(8,128)(2,1)}, f32[12,192,128]{2,1,0:T(8,128)}, bf16[4,192,128]{...) while((s32[]{:T(128)}, ...), condition=%wide.region_2.3_spmd, body=%wide.region_0.2_spmd.sunk | while | flops 1027326720 | bytes 65218820 | solution.py:126
  45.1 4.6 select_dynamic-update-slice_fusion.7
  49.7 4.0 collective-permute-start
  87.8 4.6 select_dynamic-update-slice_fusion.7
  92.4 4.0 collective-permute-start
  129.4 4.6 select_dynamic-update-slice_fusion.7
  134.1 4.0 collective-permute-start
  171.2 4.6 select_dynamic-update-slice_fusion.7
  175.8 3.7 collective-permute-start
  212.6 4.6 select_dynamic-update-slice_fusion.7
  217.2 3.7 collective-permute-start
  254.0 4.6 select_dynamic-update-slice_fusion.7
  258.6 3.7 collective-permute-start
  266.0 381.1 %while.45 = (s32[]{:T(128)}, f32[4,192,128]{1,2,0:T(8,128)}, f32[2,192,128]{1,2,0:T(8,128)}, f32[192,5184]{1,0:T(8,128)}, f32[192]{0:T(256)S(1)}, /*index=5*/pre...) while((s32[]{:T(128)}, f32[4,192,128]{1,2,0:T(8,128)}, ...), condition=%wide.region_7.8_spmd.clone, body=%wide.region_3.7_spmd.clone.sunk | while | flops 2055010048 | bytes 183801616 | solution.py:165
  272.5 3.8 fusion.55
  276.3 5.5 copy.84
  281.9 5.6 copy.85
  287.5 3.4 copy.86
  290.9 5.8 pad_add_fusion.13
  308.7 3.6 pad_maximum_fusion.5
  312.3 9.1 %copy.87 = bf16[4,27,192,128]{3,2,1,0:T(8,128)(2,1)} copy(bf16[4,27,192,128]{2,3,0,1:T(8,128)(2,1)} %pad_maximum_fusion.5) | data formatting | bytes 10616832 | tf_op jit(solution)/shard_map/while/body/eval_jaxpr/concatenate | solution.py:41
  321.4 6.3 fusion.62
  335.0 3.8 fusion.55
  338.8 5.5 copy.84
  344.4 5.6 copy.85
  350.0 3.4 copy.86
  353.4 5.8 pad_add_fusion.13
  371.2 3.6 pad_maximum_fusion.5
  374.8 9.1 %copy.87 = bf16[4,27,192,128]{3,2,1,0:T(8,128)(2,1)} copy(bf16[4,27,192,128]{2,3,0,1:T(8,128)(2,1)} %pad_maximum_fusion.5) | data formatting | bytes 10616832 | tf_op jit(solution)/shard_map/while/body/eval_jaxpr/concatenate | solution.py:41
  383.9 7.5 fusion.62
  398.7 3.8 fusion.55
  402.6 5.5 copy.84
  408.1 5.6 copy.85
  413.7 3.4 copy.86
  417.2 5.8 pad_add_fusion.13
  434.9 3.6 pad_maximum_fusion.5
  438.5 9.1 %copy.87 = bf16[4,27,192,128]{3,2,1,0:T(8,128)(2,1)} copy(bf16[4,27,192,128]{2,3,0,1:T(8,128)(2,1)} %pad_maximum_fusion.5) | data formatting | bytes 10616832 | tf_op jit(solution)/shard_map/while/body/eval_jaxpr/concatenate | solution.py:41
  447.6 7.5 fusion.62
  462.5 3.8 fusion.55
  466.3 5.5 copy.84
  471.8 5.6 copy.85
  477.4 3.4 copy.86
  480.9 5.8 pad_add_fusion.13
  498.6 3.6 pad_maximum_fusion.5
  502.2 9.1 %copy.87 = bf16[4,27,192,128]{3,2,1,0:T(8,128)(2,1)} copy(bf16[4,27,192,128]{2,3,0,1:T(8,128)(2,1)} %pad_maximum_fusion.5) | data formatting | bytes 10616832 | tf_op jit(solution)/shard_map/while/body/eval_jaxpr/concatenate | solution.py:41
  511.4 7.5 fusion.62
  526.2 3.8 fusion.55
  530.0 5.5 copy.84
  535.5 5.6 copy.85
  541.2 3.4 copy.86
  544.6 5.8 pad_add_fusion.13
  562.3 3.6 pad_maximum_fusion.5
  566.0 9.1 %copy.87 = bf16[4,27,192,128]{3,2,1,0:T(8,128)(2,1)} copy(bf16[4,27,192,128]{2,3,0,1:T(8,128)(2,1)} %pad_maximum_fusion.5) | data formatting | bytes 10616832 | tf_op jit(solution)/shard_map/while/body/eval_jaxpr/concatenate | solution.py:41
  575.1 7.5 fusion.62
  589.9 3.8 fusion.55
  593.7 5.5 copy.84
  599.3 5.6 copy.85
  604.9 3.4 copy.86
  608.3 5.8 pad_add_fusion.13
  626.1 3.6 pad_maximum_fusion.5
  629.7 9.1 %copy.87 = bf16[4,27,192,128]{3,2,1,0:T(8,128)(2,1)} copy(bf16[4,27,192,128]{2,3,0,1:T(8,128)(2,1)} %pad_maximum_fusion.5) | data formatting | bytes 10616832 | tf_op jit(solution)/shard_map/while/body/eval_jaxpr/concatenate | solution.py:41
  638.8 7.5 fusion.62
  649.0 70.2 %all-reduce.18 = f32[192]{0:T(256)S(1)} all-reduce(f32[192]{0:T(256)S(1)} %get-tuple-element.576), channel_id=3, replica_groups=mesh['segment'=4,'dp'=32] {'dp'}, use_global_device_ids=true, to_apply=%region_9.10.clone | all-reduce | flops 192 | bytes 1536
  720.7 53.0 %all-reduce.21.cloned.1.call-done = f32[192,5184]{1,0:T(8,128)} async-done(((f32[192,5184]{1,0:T(8,128)}), f32[192,5184]{1,0:T(8,128)}) %all-reduce.21.cloned.1.call-update) | async-done | bytes 3981328
  (549 shorter events, 324.6 us)
Async XLA Ops:
  7.2 766.5 %all-reduce.21.cloned.1.call-start = ((), (), s32[]{:S(2)}) async-start(), calls=%async_computation | async-start | bytes 8060928
  9.2 5.6 copy-start.13
  42.3 2.8 copy-start.8
  49.7 7.9 %collective-permute-start = (bf16[4,192,128]{2,1,0:T(8,128)(2,1)}, bf16[4,192,128]{2,1,0:T(8,128)(2,1)S(1)}, u32[]{:S(2)}, u32[]{:S(2)}) collective-permute-start(bf16[4,192,128]{2,1,0:T(8,128)(2,1)} %get-tuple-element.924), channel_id=1, source_target_pairs={{0,32},{32,64},{64,96},{1,33},{33,65},{65,97},{2,34},{34,66},{66,9... | collective-permute-start | bytes 589832 | tf_op jit(solution)/shard_map/while/body/eval_jaxpr/ppermute | solution.py:16
  84.9 2.8 copy-start.8
  92.4 6.9 collective-permute-start
  126.6 2.8 copy-start.8
  134.1 6.9 collective-permute-start
  168.3 2.8 copy-start.8
  175.8 6.6 collective-permute-start
  209.7 2.8 copy-start.8
  217.2 6.6 collective-permute-start
  251.1 2.8 copy-start.8
  258.6 6.6 collective-permute-start
  266.0 6.5 copy-start
  266.0 4.8 copy-start.9
  296.7 2.5 copy-start.1
  299.4 2.3 copy-start.2
  299.4 2.3 copy-start.3
  299.4 2.3 copy-start.4
  299.4 2.5 copy-start.5
  305.7 22.2 %collective-permute-start.1 = (f32[4,192,128]{1,2,0:T(8,128)}, f32[4,192,128]{1,2,0:T(8,128)}, u32[]{:S(2)}, u32[]{:S(2)}) collective-permute-start(f32[4,192,128]{1,2,0:T(8,128)} %slice.386), channel_id=1, source_target_pairs={{32,0},{64,32},{96,64},{33,1},{65,33},{97,65},{34,2},{66,34},{98,6... | collective-permute-start | bytes 1179656 | tf_op jit(solution)/shard_map/while/body/eval_jaxpr/ppermute | solution.py:16
  312.3 9.1 %copy-start.7 = (bf16[4,192,128]{1,2,0:T(8,128)(2,1)S(1)}, bf16[4,192,128]{1,2,0:T(8,128)(2,1)}, u32[]{:S(2)}) copy-start(bf16[4,192,128]{1,2,0:T(8,128)(2,1)} %copy-done.6) | copy-start | bytes 589828 | tf_op jit(solution)/shard_map/while
  328.5 6.5 copy-start
  328.5 4.8 copy-start.9
  359.2 2.5 copy-start.1
  361.9 2.3 copy-start.2
  361.9 2.3 copy-start.3
  361.9 2.3 copy-start.4
  361.9 2.5 copy-start.5
  368.2 23.4 %collective-permute-start.1 = (f32[4,192,128]{1,2,0:T(8,128)}, f32[4,192,128]{1,2,0:T(8,128)}, u32[]{:S(2)}, u32[]{:S(2)}) collective-permute-start(f32[4,192,128]{1,2,0:T(8,128)} %slice.386), channel_id=1, source_target_pairs={{32,0},{64,32},{96,64},{33,1},{65,33},{97,65},{34,2},{66,34},{98,6... | collective-permute-start | bytes 1179656 | tf_op jit(solution)/shard_map/while/body/eval_jaxpr/ppermute | solution.py:16
  374.8 9.1 %copy-start.7 = (bf16[4,192,128]{1,2,0:T(8,128)(2,1)S(1)}, bf16[4,192,128]{1,2,0:T(8,128)(2,1)}, u32[]{:S(2)}) copy-start(bf16[4,192,128]{1,2,0:T(8,128)(2,1)} %copy-done.6) | copy-start | bytes 589828 | tf_op jit(solution)/shard_map/while
  392.3 6.5 copy-start
  392.3 4.8 copy-start.9
  422.9 2.5 copy-start.1
  425.6 2.3 copy-start.2
  425.6 2.3 copy-start.3
  425.6 2.3 copy-start.4
  425.7 2.5 copy-start.5
  431.9 23.4 %collective-permute-start.1 = (f32[4,192,128]{1,2,0:T(8,128)}, f32[4,192,128]{1,2,0:T(8,128)}, u32[]{:S(2)}, u32[]{:S(2)}) collective-permute-start(f32[4,192,128]{1,2,0:T(8,128)} %slice.386), channel_id=1, source_target_pairs={{32,0},{64,32},{96,64},{33,1},{65,33},{97,65},{34,2},{66,34},{98,6... | collective-permute-start | bytes 1179656 | tf_op jit(solution)/shard_map/while/body/eval_jaxpr/ppermute | solution.py:16
  438.5 9.1 %copy-start.7 = (bf16[4,192,128]{1,2,0:T(8,128)(2,1)S(1)}, bf16[4,192,128]{1,2,0:T(8,128)(2,1)}, u32[]{:S(2)}) copy-start(bf16[4,192,128]{1,2,0:T(8,128)(2,1)} %copy-done.6) | copy-start | bytes 589828 | tf_op jit(solution)/shard_map/while
  456.0 6.5 copy-start
  456.0 4.8 copy-start.9
  486.7 2.5 copy-start.1
  489.3 2.3 copy-start.2
  489.4 2.3 copy-start.3
  489.4 2.3 copy-start.4
  489.4 2.5 copy-start.5
  495.6 23.4 %collective-permute-start.1 = (f32[4,192,128]{1,2,0:T(8,128)}, f32[4,192,128]{1,2,0:T(8,128)}, u32[]{:S(2)}, u32[]{:S(2)}) collective-permute-start(f32[4,192,128]{1,2,0:T(8,128)} %slice.386), channel_id=1, source_target_pairs={{32,0},{64,32},{96,64},{33,1},{65,33},{97,65},{34,2},{66,34},{98,6... | collective-permute-start | bytes 1179656 | tf_op jit(solution)/shard_map/while/body/eval_jaxpr/ppermute | solution.py:16
  502.2 9.1 %copy-start.7 = (bf16[4,192,128]{1,2,0:T(8,128)(2,1)S(1)}, bf16[4,192,128]{1,2,0:T(8,128)(2,1)}, u32[]{:S(2)}) copy-start(bf16[4,192,128]{1,2,0:T(8,128)(2,1)} %copy-done.6) | copy-start | bytes 589828 | tf_op jit(solution)/shard_map/while
  519.7 6.5 copy-start
  519.7 4.8 copy-start.9
  550.4 2.5 copy-start.1
  553.1 2.3 copy-start.2
  553.1 2.5 copy-start.5
  559.3 23.4 %collective-permute-start.1 = (f32[4,192,128]{1,2,0:T(8,128)}, f32[4,192,128]{1,2,0:T(8,128)}, u32[]{:S(2)}, u32[]{:S(2)}) collective-permute-start(f32[4,192,128]{1,2,0:T(8,128)} %slice.386), channel_id=1, source_target_pairs={{32,0},{64,32},{96,64},{33,1},{65,33},{97,65},{34,2},{66,34},{98,6... | collective-permute-start | bytes 1179656 | tf_op jit(solution)/shard_map/while/body/eval_jaxpr/ppermute | solution.py:16
  566.0 9.1 %copy-start.7 = (bf16[4,192,128]{1,2,0:T(8,128)(2,1)S(1)}, bf16[4,192,128]{1,2,0:T(8,128)(2,1)}, u32[]{:S(2)}) copy-start(bf16[4,192,128]{1,2,0:T(8,128)(2,1)} %copy-done.6) | copy-start | bytes 589828 | tf_op jit(solution)/shard_map/while
  583.4 6.5 copy-start
  583.4 4.8 copy-start.9
  614.1 2.5 copy-start.1
  616.8 2.5 copy-start.5
  623.0 23.4 %collective-permute-start.1 = (f32[4,192,128]{1,2,0:T(8,128)}, f32[4,192,128]{1,2,0:T(8,128)}, u32[]{:S(2)}, u32[]{:S(2)}) collective-permute-start(f32[4,192,128]{1,2,0:T(8,128)} %slice.386), channel_id=1, source_target_pairs={{32,0},{64,32},{96,64},{33,1},{65,33},{97,65},{34,2},{66,34},{98,6... | collective-permute-start | bytes 1179656 | tf_op jit(solution)/shard_map/while/body/eval_jaxpr/ppermute | solution.py:16
  629.7 9.1 %copy-start.7 = (bf16[4,192,128]{1,2,0:T(8,128)(2,1)S(1)}, bf16[4,192,128]{1,2,0:T(8,128)(2,1)}, u32[]{:S(2)}) copy-start(bf16[4,192,128]{1,2,0:T(8,128)(2,1)} %copy-done.6) | copy-start | bytes 589828 | tf_op jit(solution)/shard_map/while
  647.2 72.7 %copy-start.12 = (bf16[12,192,128]{2,1,0:T(8,128)(2,1)S(1)}, bf16[12,192,128]{2,1,0:T(8,128)(2,1)}, u32[]{:S(2)}) copy-start(bf16[12,192,128]{2,1,0:T(8,128)(2,1)} %get-tuple-element.572) | copy-start | bytes 1769476
  (24 other events, 39.1 us)
Sparse Core Ops, SparseCore 0:
  647.3 126.3 all-reduce.20
where the time goes:
time: 789 us; the launch traced here: 782 us
  local copies, waits for them, and re-layouts  400 us (51%)
  other arithmetic  121 us (15%)
  matrix products  81.7 us (10%)
  blocking collectives  70.2 us (9%)
  waiting for transfers between devices  60.6 us (8%)
  starting transfers between devices  30.9 us (4%)
  between operations  15.4 us (2%)
    while x252, local copies, waits for them, and re-layouts  136 us
    reshape x48, local copies, waits for them, and re-layouts, make_patches(): jnp.stack([padded[:, :, row:row + TILE_H, col:col + TILE_W].reshape(frame...  84.5 us
    concatenate x12, local copies, waits for them, and re-layouts, make_patches(): jnp.concatenate([spatial[tap:tap + blocks] for tap in range(3)], axis=1)  71.1 us
    unnamed x1, blocking collectives  70.2 us
    unnamed x2, waiting for transfers between devices  53 us
    dot_general x6, matrix products, section_backward(): jnp.einsum('fop,fkp->ok', grad_conv, patches, preferred_element_type=jnp....  44 us
    add_any x6, other arithmetic, make_patches(): spatial[tap:tap + blocks]  34.7 us
    ppermute x12, starting transfers between devices, shifted(): return lax.ppermute(block, axis, route)  30.8 us
  transfers between devices with their start and end apart: 13, of which 7 were waited for; matrix products, arithmetic and copies ran while one was open for 18% of the time, Pallas kernels for 0%

commit v1 on v0

v1 whole, which is shorter than its diff:
```python
import jax
import jax.numpy as jnp
from jax import lax
from jax.experimental import pallas as pl
from jax.experimental.pallas import tpu as pltpu
from jax.sharding import PartitionSpec as P

TILE_H = 8
TILE_W = 16
EPS = 1e-06

F = 9
C = 192
PIX = 128
K3 = 9 * C
KK = 27 * C
N0 = 1408
N1 = 1280
HALF = N0 + N1

BF = jnp.bfloat16
F32 = jnp.float32
NT = (((1,), (1,)), ((), ()))


def tap_masks():
    lane = lax.broadcasted_iota(jnp.int32, (1, PIX), 1)
    col = lane & (TILE_W - 1)
    masks = []
    for a in range(3):
        for b in range(3):
            pos = lane + TILE_W * (a - 1)
            ok = (col + (b - 1) >= 0) & (col + (b - 1) < TILE_W) & (pos >= 0) & (pos < PIX)
            masks.append(jnp.where(ok, 1.0, 0.0).astype(BF))
    return masks


def store_patches(dst, base, frame):
    masks = tap_masks()
    for a in range(3):
        for b in range(3):
            k = a * 3 + b
            shift = (-(TILE_W * (a - 1) + (b - 1))) % PIX
            value = frame if shift == 0 else pltpu.roll(frame, shift, 1) * masks[k]
            dst[pl.ds(base + k * C, C), :] = value


def kernel(groups, video, weight, gain, cot, feat, dweight, dgain,
           xin, dyin, dysend, fac, scales, gain_b, gain_acc, sp, dp_, wt, dconv_all, dconv_perm,
           a0, a1, b0, b1, c0, c1, d0, d1, f0, f1, g0, g1,
           fsend, frecv, bsend, brecv, s0send, s0recv, s1send, s1recv, s2send, s2recv):
    seg = lax.axis_index("segment")
    d = lax.axis_index("dp")
    core = lax.rem(d, 2)
    xc = lax.rem(lax.div(d, 2), 4)
    zc = lax.div(d, 8)

    def dev(z, x, c):
        return {"dp": (z * 4 + x) * 2 + c}

    def put(src, dst, ssem, rsem, where):
        return pltpu.make_async_remote_copy(
            src_ref=src, dst_ref=dst, send_sem=ssem, recv_sem=rsem,
            device_id=where, device_id_type=pl.DeviceIdType.MESH)

    barrier = pltpu.get_barrier_semaphore()

    def greet(where):
        pl.semaphore_signal(barrier, inc=1, device_id=where, device_id_type=pl.DeviceIdType.MESH)

    greet({"segment": lax.rem(seg + 1, 4)})
    greet({"segment": lax.rem(seg + 3, 4)})
    greet(dev(zc, xc, 1 - core))
    for r in range(1, 4):
        for c in range(2):
            greet(dev(lax.rem(zc + r, 4), xc, c))
            greet(dev(zc, lax.rem(xc + r, 4), c))

    count = groups[0] * 4 - 3

    def keep(i):
        return jnp.where(i < count, 1.0, 0.0).astype(F32)

    zero_patch = jnp.zeros((K3, PIX), BF)
    sp[0:K3, :] = zero_patch
    sp[K3:2 * K3, :] = zero_patch
    sp[11 * K3:, :] = jnp.zeros((C, PIX), BF)
    dp_[9 * K3:10 * K3, :] = zero_patch
    dp_[10 * K3:11 * K3, :] = zero_patch
    gain_b[...] = jnp.broadcast_to(gain[...], (PIX, C)).T
    gain_acc[...] = jnp.zeros((C, PIX), F32)

    def transpose_weight():
        for tap in range(27):
            wt[:, (26 - tap) * C:(27 - tap) * C] = weight[:, tap * C:(tap + 1) * C].T

    @pl.when(seg == 0)
    def _():
        for i in range(F):
            xin[i] = (video[i].astype(F32) * keep(i)).astype(BF)

    @pl.when(seg == 3)
    def _():
        for i in range(F):
            dyin[i] = cot[i]

    @pl.when(seg >= 2)
    def _():
        transpose_weight()

    pl.semaphore_wait(barrier, 15)

    def fwd_copy(i):
        return put(feat.at[i], xin.at[i], fsend.at[i], frecv.at[i], {"segment": lax.rem(seg + 1, 4)})

    def bwd_copy(i):
        return put(dysend.at[i], dyin.at[i], bsend.at[i], brecv.at[i], {"segment": lax.rem(seg + 3, 4)})

    def forward(i, carry):
        @pl.when(seg > 0)
        def _():
            fwd_copy(i).wait_recv()

        x = xin[i].astype(F32)
        scale = lax.rsqrt(jnp.sum(x * x, axis=0, keepdims=True) * (1.0 / C) + EPS)
        scales[i] = scale
        normed = (x * scale * gain_b[...]).astype(BF)
        store_patches(sp, pl.multiple_of((i + 2) * K3, 64), normed)
        window = sp[pl.ds(pl.multiple_of(i * K3, 64), KK), :]
        conv = jnp.dot(weight[...], window, preferred_element_type=F32)
        sig = 1.0 / (1.0 + jnp.exp(-conv))
        feat[i] = ((x + conv * sig) * keep(i)).astype(BF)

        @pl.when(seg < 3)
        def _():
            fwd_copy(i).start()

        fac[i] = sig * (1.0 + conv * (1.0 - sig))
        return carry

    lax.fori_loop(0, F, forward, 0)

    @pl.when(seg < 2)
    def _():
        transpose_weight()

    def backward(n, carry):
        i = F - 1 - n

        @pl.when(seg < 3)
        def _():
            bwd_copy(i).wait_recv()

        dz = dyin[i].astype(F32) * keep(i)
        dconv = (dz * fac[i]).astype(BF)
        dconv_all[:, pl.ds(pl.multiple_of(i * PIX, PIX), PIX)] = dconv
        store_patches(dp_, pl.multiple_of(i * K3, 64), dconv)
        window = dp_[pl.ds(pl.multiple_of(i * K3, 64), KK), :]
        dnormed = jnp.dot(wt[...], window, preferred_element_type=F32)
        x = xin[i].astype(F32)
        scale = scales[i]
        gx = dnormed * gain_b[...]
        inner = jnp.sum(gx * x, axis=0, keepdims=True)
        dx = scale * gx - x * (scale * scale * scale * inner * (1.0 / C)) + dz
        dysend[i] = dx.astype(BF)

        @pl.when(seg > 0)
        def _():
            bwd_copy(i).start()

        gain_acc[...] += dnormed * x * scale
        return carry

    lax.fori_loop(0, F, backward, 0)

    row = lax.broadcasted_iota(jnp.int32, (C, C), 0)
    colm = lax.broadcasted_iota(jnp.int32, (C, C), 1)
    blk = lax.div(row, 12)
    source = (lax.rem(blk, 4) * 4 + lax.div(blk, 4)) * 12 + lax.rem(row, 12)
    perm = jnp.where(colm == source, 1.0, 0.0).astype(BF)
    dconv_perm[...] = jnp.dot(perm, dconv_all[...], preferred_element_type=F32).astype(BF)
    gain_perm = jnp.dot(perm, gain_acc[...].astype(BF), preferred_element_type=F32).astype(BF)

    def stage0(h, half):
        src, dst = ((a0, b0), (a1, b1))[h]
        return put(src.at[half], dst, s0send.at[h], s0recv.at[h], dev(zc, xc, 1 - core))

    def weight_part(lhs, dst, half, start, chunks):
        off = 0
        for size in chunks:
            col = pl.multiple_of(half * HALF + start + off, 128)
            rhs = jnp.concatenate([sp[pl.ds(f * K3 + col, size), :] for f in range(F)], axis=1)
            dst[half, :, off:off + size] = lax.dot_general(
                lhs[...], rhs, NT, preferred_element_type=F32).astype(BF)
            off += size

    def weight_half(n, carry):
        half = jnp.where(n == 0, 1 - core, core)
        weight_part(dconv_all, a0, half, 0, (768, 640))

        @pl.when(n == 0)
        def _():
            stage0(0, half).start()

        weight_part(dconv_perm, a1, half, N0, (640, 640))
        a1[half, :, N1 - 128:] = jnp.where(half == 1, gain_perm, a1[half, :, N1 - 128:])

        @pl.when(n == 0)
        def _():
            stage0(1, half).start()

        return carry

    lax.fori_loop(0, 2, weight_half, 0)

    def stage1(h, r):
        if h == 0:
            to = lax.rem(zc + r, 4)
            return put(c0.at[to], d0.at[r - 1], s1send.at[h, r - 1], s1recv.at[h, r - 1], dev(to, xc, core))
        to = lax.rem(xc + r, 4)
        return put(c1.at[to], d1.at[r - 1], s1send.at[h, r - 1], s1recv.at[h, r - 1], dev(zc, to, core))

    for h in range(2):
        stage0(h, 1 - core).wait_recv()
        mine, other, out = ((a0, b0, c0), (a1, b1, c1))[h]
        for q in range(4):
            rows = slice(q * 48, (q + 1) * 48)
            out[q] = (mine[core, rows, :].astype(F32) + other[rows, :].astype(F32)).astype(BF)
        for r in (2, 1, 3):
            stage1(h, r).start()

    prow = lax.broadcasted_iota(jnp.int32, (64, 48), 0)
    pcol = lax.broadcasted_iota(jnp.int32, (64, 48), 1)
    spread = jnp.where((lax.rem(prow, 8) < 6) & (pcol == lax.div(prow, 8) * 6 + lax.rem(prow, 8)), 1.0, 0.0).astype(BF)

    def stage2(h, r, c):
        if h == 0:
            to = lax.rem(xc + r, 4)
            where, src, dst = dev(zc, to, c), f0, g0
        else:
            to = lax.rem(zc + r, 4)
            where, src, dst = dev(to, xc, c), f1, g1
        slot = r * 2 + jnp.where(c == core, 0, 1)
        return put(src.at[to * 2 + c], dst.at[core * 4 + r], s2send.at[h, slot], s2recv.at[h, slot], where)

    for h in range(2):
        own, got, out = ((c0, d0, f0), (c1, d1, f1))[h]
        me = zc if h == 0 else xc
        for r in range(1, 4):
            stage1(h, r).wait_recv()
        total = own[me].astype(F32)
        for r in range(3):
            total = total + got[r].astype(F32)
        spaced = jnp.dot(spread, total.astype(BF), preferred_element_type=F32).astype(BF)
        for k in range(8):
            out[k] = spaced[k * 8:(k + 1) * 8, :]
        for r in (2, 1, 3):
            stage2(h, r, core).start()
            stage2(h, r, 1 - core).start()
        stage2(h, 0, 1 - core).start()

    def stage2_wait(h, r, c):
        slot = r * 2 + jnp.where(c == core, 0, 1)
        src, dst = ((f0, g0), (f1, g1))[h]
        where = dev(zc, lax.rem(xc + r, 4), c) if h == 0 else dev(lax.rem(zc + r, 4), xc, c)
        return put(src.at[0], dst.at[c * 4 + r], s2send.at[h, slot], s2recv.at[h, slot], where)

    for h in range(2):
        src, dst = ((f0, g0), (f1, g1))[h]
        mine = (xc if h == 0 else zc) * 2 + core
        dst[core * 4] = src[mine]
        for r in range(4):
            if r:
                stage2_wait(h, r, core).wait_recv()
            stage2_wait(h, r, 1 - core).wait_recv()
        for c in range(2):
            total = dst[c * 4].astype(F32)
            for r in range(1, 4):
                total = total + dst[c * 4 + r].astype(F32)
            start = c * HALF + (0 if h == 0 else N0)
            size = min(N0 if h == 0 else N1, KK - start)
            dweight[:, start:start + size] = total[0:6, 0:size]
            if h == 1 and c == 1:
                per_row = jnp.sum(total[:, N1 - 128:], axis=1, keepdims=True)
                r8 = lax.broadcasted_iota(jnp.int32, (8, 128), 0)
                l8 = lax.broadcasted_iota(jnp.int32, (8, 128), 1)
                line = jnp.sum(jnp.where(r8 == l8, per_row, 0.0), axis=0, keepdims=True)
                dgain[...] = line[:, 0:6]

    @pl.when(seg < 3)
    def _():
        def done(i, carry):
            fwd_copy(i).wait_send()
            return carry
        lax.fori_loop(0, F, done, 0)

    @pl.when(seg > 0)
    def _():
        def done(i, carry):
            bwd_copy(i).wait_send()
            return carry
        lax.fori_loop(0, F, done, 0)

    for h in range(2):
        stage0(h, 1 - core).wait_send()
        for r in range(1, 4):
            stage1(h, r).wait_send()
            stage2_wait(h, r, core).wait_send()
            stage2_wait(h, r, 1 - core).wait_send()
        stage2_wait(h, 0, 1 - core).wait_send()


def body(video_clips, conv_weight, norm_gain, cotangent, clip_groups):
    vmem = pl.BlockSpec(memory_space=pltpu.VMEM)
    smem = pl.BlockSpec(memory_space=pltpu.SMEM)
    dma = pltpu.SemaphoreType.DMA
    feat, dweight, dgain = pl.pallas_call(
        kernel,
        out_shape=(
            jax.ShapeDtypeStruct((F, C, PIX), BF),
            jax.ShapeDtypeStruct((6, KK), F32),
            jax.ShapeDtypeStruct((1, 6), F32),
        ),
        in_specs=[smem, vmem, vmem, vmem, vmem],
        out_specs=(vmem, vmem, vmem),
        scratch_shapes=[
            pltpu.VMEM((F, C, PIX), BF),
            pltpu.VMEM((F, C, PIX), BF),
            pltpu.VMEM((F, C, PIX), BF),
            pltpu.VMEM((F, C, PIX), F32),
            pltpu.VMEM((F, 1, PIX), F32),
            pltpu.VMEM((C, PIX), F32),
            pltpu.VMEM((C, PIX), F32),
            pltpu.VMEM((11 * K3 + C, PIX), BF),
            pltpu.VMEM((11 * K3, PIX), BF),
            pltpu.VMEM((C, KK), BF),
            pltpu.VMEM((C, F * PIX), BF),
            pltpu.VMEM((C, F * PIX), BF),
            pltpu.VMEM((2, C, N0), BF),
            pltpu.VMEM((2, C, N1), BF),
            pltpu.VMEM((C, N0), BF),
            pltpu.VMEM((C, N1), BF),
            pltpu.VMEM((4, 48, N0), BF),
            pltpu.VMEM((4, 48, N1), BF),
            pltpu.VMEM((3, 48, N0), BF),
            pltpu.VMEM((3, 48, N1), BF),
            pltpu.VMEM((8, 8, N0), BF),
            pltpu.VMEM((8, 8, N1), BF),
            pltpu.VMEM((8, 8, N0), BF),
            pltpu.VMEM((8, 8, N1), BF),
            dma((F,)), dma((F,)), dma((F,)), dma((F,)),
            dma((2,)), dma((2,)),
            dma((2, 3)), dma((2, 3)),
            dma((2, 8)), dma((2, 8)),
        ],
        compiler_params=pltpu.CompilerParams(
            collective_id=0, has_side_effects=True, vmem_limit_bytes=56 << 20),
    )(clip_groups, video_clips[0], conv_weight[0], norm_gain, cotangent[0])
    return (feat[None, None], dweight[None], dgain)


def solution(mesh):
    placed = (
        P("dp", None, None, None),
        P("segment", None, None),
        P("segment", None),
        P("dp", None, None, None),
        P("dp"),
    )
    return jax.shard_map(
        body,
        mesh=mesh,
        in_specs=placed,
        out_specs=(
            P("segment", "dp", None, None, None),
            P("segment", "dp", None),
            P("segment", "dp"),
        ),
        check_vma=False,
    )
```

time: 789 us -> 77.7 us (0.10)
  local copies, waits for them, and re-layouts: 400 us -> 4.6 us
  other arithmetic: 121 us -> 0 us
  matrix products: 81.7 us -> 0 us
  Pallas kernels: 0 us -> 71.6 us
  blocking collectives: 70.2 us -> 0 us
  waiting for transfers between devices: 60.6 us -> 0 us
  starting transfers between devices: 30.9 us -> 0 us
  between operations: 15.4 us -> 1.29 us
    while x252 -> x0, local copies, waits for them, and re-layouts: 136 us -> none
    reshape x48 -> x0, local copies, waits for them, and re-layouts: 84.5 us -> none  [make_patches(): jnp.stack([padded[:, :, row:row + TILE_H, col:col + TILE_W].reshape(frame...]
    dot_general x18 -> x0, matrix products: 81.7 us -> none  [the longest x6 44 us: section_backward(): jnp.einsum('fop,fkp->ok', grad_conv, patches, preferred_element_type=jnp....]
    concatenate x13 -> x0, local copies, waits for them, and re-layouts: 72.1 us -> none  [the longest x12 71.1 us: make_patches(): jnp.concatenate([spatial[tap:tap + blocks] for tap in range(3)], axis=1)]
    pallas_call x0 -> x1, Pallas kernels: none -> 71.6 us  [body(): pl.pallas_call(kernel, out_shape=(jax.ShapeDtypeStruct((F, C, PIX), BF),...]
    unnamed x1 -> x0, blocking collectives: 70.2 us -> none
    unnamed x2 -> x0, waiting for transfers between devices: 53 us -> none
    add_any x24 -> x0, other arithmetic: 52.6 us -> none  [the longest x6 34.7 us: make_patches(): spatial[tap:tap + blocks]]
  transfers between devices with their start and end apart: 13 -> 0, of which waited for: 7 -> 0; matrix products, arithmetic and copies ran while one was open for 18% -> 0% of each run, Pallas kernels for 0% -> 0%
where the time goes in v1:
time: 77.7 us; the launch traced here: 77.5 us
  Pallas kernels  71.6 us (92%)
  local copies, waits for them, and re-layouts  4.6 us (6%)
  between operations  1.29 us (2%)
    pallas_call x1, Pallas kernels, body(): pl.pallas_call(kernel, out_shape=(jax.ShapeDtypeStruct((F, C, PIX), BF),...  71.6 us
    unnamed x3, local copies, waits for them, and re-layouts  4.6 us

profile of v1, /device:TPU:1, one launch (start us, length us, event | category | flops | bytes accessed | tf_op | source)
XLA Modules:
  0.0 77.5 jit_solution(16462514885166319074)
XLA Ops:
  1.3 71.6 %shard_map.76 = (bf16[9,192,128]{2,1,0:T(8,128)(2,1)}, f32[6,5184]{1,0:T(8,128)}, f32[1,6]{1,0:T(1,128)}) custom-call(s32[1]{0:T(128)S(6)} %copy.11.groups, bf16[9,192,128]{2,1,0:T(8,128)(2,1)} %bitcast.7, bf16[192,5184]{1,0:T(8,128)(2,1)} %bitcast.5, f32[1,192]{1,0:T(1,128)} %gain.1, bf16[9,192,128]{2,1,0:T(8,128)(2,1)} %bitcast.8), custom_call_target="tpu_custom_call" | custom-call | tf_op jit(solution)/shard_map/pallas_call | solution.py:317
  72.9 1.7 %copy.8 = f32[1,6,5184]{2,0,1:T(1,128)} copy(f32[1,6,5184]{2,1,0:T(8,128)} %bitcast.9) | data formatting | bytes 248832
  74.6 1.8 %copy.12 = bf16[1,1,9,192,128]{4,3,2,1,0:T(8,128)(2,1)} copy(bf16[1,1,9,192,128]{4,3,2,1,0:T(8,128)(2,1)} %bitcast.6) | data formatting | bytes 884736
  76.4 1.1 %copy.13 = f32[1,6]{1,0:T(1,128)} copy(f32[1,6]{1,0:T(1,128)} %get-tuple-element.17) | data formatting | bytes 48

commit v2 on v1

--- a/solution.py
+++ b/solution.py
@@ -37,18 +37,22 @@
 
 def store_patches(dst, base, frame):
     masks = tap_masks()
+    values = []
     for a in range(3):
         for b in range(3):
             k = a * 3 + b
             shift = (-(TILE_W * (a - 1) + (b - 1))) % PIX
-            value = frame if shift == 0 else pltpu.roll(frame, shift, 1) * masks[k]
-            dst[pl.ds(base + k * C, C), :] = value
-
-
-def kernel(groups, video, weight, gain, cot, feat, dweight, dgain,
+            values.append(frame if shift == 0 else pltpu.roll(frame, shift, 1) * masks[k])
+    patches = jnp.concatenate(values, axis=0)
+    dst[pl.ds(base, K3), :] = patches
+    return patches
+
+
+def kernel(groups, video, weight_hbm, gain, cot, feat_hbm, dweight_hbm, dgain_hbm,
+           weight, feat, video_v, dweight, dgain, pre,
            xin, dyin, dysend, fac, scales, gain_b, gain_acc, sp, dp_, wt, dconv_all, dconv_perm,
            a0, a1, b0, b1, c0, c1, d0, d1, f0, f1, g0, g1,
-           fsend, frecv, bsend, brecv, s0send, s0recv, s1send, s1recv, s2send, s2recv):
+           insem, outsem, featsem, fsend, frecv, bsend, brecv, s0send, s0recv, s1send, s1recv, s2send, s2recv):
     seg = lax.axis_index("segment")
     d = lax.axis_index("dp")
     core = lax.rem(d, 2)
@@ -62,6 +66,22 @@
         return pltpu.make_async_remote_copy(
             src_ref=src, dst_ref=dst, send_sem=ssem, recv_sem=rsem,
             device_id=where, device_id_type=pl.DeviceIdType.MESH)
+
+    early = pltpu.make_async_copy(weight_hbm.at[:, 2 * K3:], weight.at[:, 2 * K3:], insem.at[0])
+    late = pltpu.make_async_copy(weight_hbm.at[:, :2 * K3], weight.at[:, :2 * K3], insem.at[1])
+    clip = pltpu.make_async_copy(video, video_v, insem.at[2])
+    target = pltpu.make_async_copy(cot, dyin, insem.at[2])
+
+    @pl.when(seg == 0)
+    def _():
+        clip.start()
+
+    early.start()
+    late.start()
+
+    @pl.when(seg == 3)
+    def _():
+        target.start()
 
     barrier = pltpu.get_barrier_semaphore()
 
@@ -85,36 +105,39 @@
     sp[0:K3, :] = zero_patch
     sp[K3:2 * K3, :] = zero_patch
     sp[11 * K3:, :] = jnp.zeros((C, PIX), BF)
-    dp_[9 * K3:10 * K3, :] = zero_patch
-    dp_[10 * K3:11 * K3, :] = zero_patch
+    dp_[0:K3, :] = zero_patch
+    dp_[K3:2 * K3, :] = zero_patch
+    pre[...] = jnp.zeros((C, PIX), F32)
     gain_b[...] = jnp.broadcast_to(gain[...], (PIX, C)).T
     gain_acc[...] = jnp.zeros((C, PIX), F32)
 
     def transpose_weight():
         for tap in range(27):
-            wt[:, (26 - tap) * C:(27 - tap) * C] = weight[:, tap * C:(tap + 1) * C].T
+            to = (tap // 9) * 9 + 8 - tap % 9
+            wt[:, to * C:(to + 1) * C] = weight[:, tap * C:(tap + 1) * C].T
 
     @pl.when(seg == 0)
     def _():
+        clip.wait()
         for i in range(F):
-            xin[i] = (video[i].astype(F32) * keep(i)).astype(BF)
-
-    @pl.when(seg == 3)
-    def _():
-        for i in range(F):
-            dyin[i] = cot[i]
+            xin[i] = (video_v[i].astype(F32) * keep(i)).astype(BF)
+
+    early.wait()
+    late.wait()
 
     @pl.when(seg >= 2)
     def _():
         transpose_weight()
 
-    pl.semaphore_wait(barrier, 15)
 
     def fwd_copy(i):
         return put(feat.at[i], xin.at[i], fsend.at[i], frecv.at[i], {"segment": lax.rem(seg + 1, 4)})
 
     def bwd_copy(i):
         return put(dysend.at[i], dyin.at[i], bsend.at[i], brecv.at[i], {"segment": lax.rem(seg + 3, 4)})
+
+    def keep_copy(i):
+        return pltpu.make_async_copy(feat.at[i], feat_hbm.at[i], featsem.at[i])
 
     def forward(i, carry):
         @pl.when(seg > 0)
@@ -125,17 +148,23 @@
         scale = lax.rsqrt(jnp.sum(x * x, axis=0, keepdims=True) * (1.0 / C) + EPS)
         scales[i] = scale
         normed = (x * scale * gain_b[...]).astype(BF)
-        store_patches(sp, pl.multiple_of((i + 2) * K3, 64), normed)
-        window = sp[pl.ds(pl.multiple_of(i * K3, 64), KK), :]
-        conv = jnp.dot(weight[...], window, preferred_element_type=F32)
+        patches = store_patches(sp, pl.multiple_of((i + 2) * K3, 64), normed)
+        conv = pre[...] + jnp.dot(weight[:, 2 * K3:], patches, preferred_element_type=F32)
         sig = 1.0 / (1.0 + jnp.exp(-conv))
         feat[i] = ((x + conv * sig) * keep(i)).astype(BF)
 
+        @pl.when(i == 0)
+        def _():
+            pl.semaphore_wait(barrier, 15)
+
         @pl.when(seg < 3)
         def _():
             fwd_copy(i).start()
 
+        keep_copy(i).start()
         fac[i] = sig * (1.0 + conv * (1.0 - sig))
+        window = sp[pl.ds(pl.multiple_of((i + 1) * K3, 64), 2 * K3), :]
+        pre[...] = jnp.dot(weight[:, :2 * K3], window, preferred_element_type=F32)
         return carry
 
     lax.fori_loop(0, F, forward, 0)
@@ -143,6 +172,12 @@
     @pl.when(seg < 2)
     def _():
         transpose_weight()
+
+    pre[...] = jnp.zeros((C, PIX), F32)
+
+    @pl.when(seg == 3)
+    def _():
+        target.wait()
 
     def backward(n, carry):
         i = F - 1 - n
@@ -154,9 +189,8 @@
         dz = dyin[i].astype(F32) * keep(i)
         dconv = (dz * fac[i]).astype(BF)
         dconv_all[:, pl.ds(pl.multiple_of(i * PIX, PIX), PIX)] = dconv
-        store_patches(dp_, pl.multiple_of(i * K3, 64), dconv)
-        window = dp_[pl.ds(pl.multiple_of(i * K3, 64), KK), :]
-        dnormed = jnp.dot(wt[...], window, preferred_element_type=F32)
+        patches = store_patches(dp_, pl.multiple_of((n + 2) * K3, 64), dconv)
+        dnormed = pre[...] + jnp.dot(wt[:, 2 * K3:], patches, preferred_element_type=F32)
         x = xin[i].astype(F32)
         scale = scales[i]
         gx = dnormed * gain_b[...]
@@ -169,6 +203,8 @@
             bwd_copy(i).start()
 
         gain_acc[...] += dnormed * x * scale
+        window = dp_[pl.ds(pl.multiple_of((n + 1) * K3, 64), 2 * K3), :]
+        pre[...] = jnp.dot(wt[:, :2 * K3], window, preferred_element_type=F32)
         return carry
 
     lax.fori_loop(0, F, backward, 0)
@@ -279,13 +315,25 @@
                 total = total + dst[c * 4 + r].astype(F32)
             start = c * HALF + (0 if h == 0 else N0)
             size = min(N0 if h == 0 else N1, KK - start)
-            dweight[:, start:start + size] = total[0:6, 0:size]
+            for j in range(6):
+                dweight[j, :, start:start + size] = total[j:j + 1, 0:size]
             if h == 1 and c == 1:
                 per_row = jnp.sum(total[:, N1 - 128:], axis=1, keepdims=True)
                 r8 = lax.broadcasted_iota(jnp.int32, (8, 128), 0)
                 l8 = lax.broadcasted_iota(jnp.int32, (8, 128), 1)
                 line = jnp.sum(jnp.where(r8 == l8, per_row, 0.0), axis=0, keepdims=True)
-                dgain[...] = line[:, 0:6]
+                dgain[...] = line
+
+    results = (pltpu.make_async_copy(dweight, dweight_hbm, outsem.at[0]),
+               pltpu.make_async_copy(dgain, dgain_hbm, outsem.at[1]))
+    for result in results:
+        result.start()
+
+    def kept(i, carry):
+        keep_copy(i).wait()
+        return carry
+
+    lax.fori_loop(0, F, kept, 0)
 
     @pl.when(seg < 3)
     def _():
@@ -308,22 +356,37 @@
             stage2_wait(h, r, core).wait_send()
             stage2_wait(h, r, 1 - core).wait_send()
         stage2_wait(h, 0, 1 - core).wait_send()
+    for result in results:
+        result.wait()
+
+
+def hand_over(feat, dweight, dgain, feat_out, dweight_out, dgain_out):
+    feat_out[...] = feat[...]
+    dweight_out[...] = dweight[...]
+    dgain_out[...] = dgain[:, 0:6]
 
 
 def body(video_clips, conv_weight, norm_gain, cotangent, clip_groups):
     vmem = pl.BlockSpec(memory_space=pltpu.VMEM)
+    hbm = pl.BlockSpec(memory_space=pl.ANY)
     smem = pl.BlockSpec(memory_space=pltpu.SMEM)
     dma = pltpu.SemaphoreType.DMA
     feat, dweight, dgain = pl.pallas_call(
         kernel,
         out_shape=(
             jax.ShapeDtypeStruct((F, C, PIX), BF),
-            jax.ShapeDtypeStruct((6, KK), F32),
-            jax.ShapeDtypeStruct((1, 6), F32),
+            jax.ShapeDtypeStruct((6, 1, KK), F32),
+            jax.ShapeDtypeStruct((1, 128), F32),
         ),
-        in_specs=[smem, vmem, vmem, vmem, vmem],
-        out_specs=(vmem, vmem, vmem),
+        in_specs=[smem, hbm, hbm, vmem, hbm],
+        out_specs=(hbm, hbm, hbm),
         scratch_shapes=[
+            pltpu.VMEM((C, KK), BF),
+            pltpu.VMEM((F, C, PIX), BF),
+            pltpu.VMEM((F, C, PIX), BF),
+            pltpu.VMEM((6, 1, KK), F32),
+            pltpu.VMEM((1, 128), F32),
+            pltpu.VMEM((C, PIX), F32),
             pltpu.VMEM((F, C, PIX), BF),
             pltpu.VMEM((F, C, PIX), BF),
             pltpu.VMEM((F, C, PIX), BF),
@@ -348,6 +411,7 @@
             pltpu.VMEM((8, 8, N1), BF),
             pltpu.VMEM((8, 8, N0), BF),
             pltpu.VMEM((8, 8, N1), BF),
+            dma((3,)), dma((2,)), dma((F,)),
             dma((F,)), dma((F,)), dma((F,)), dma((F,)),
             dma((2,)), dma((2,)),
             dma((2, 3)), dma((2, 3)),
@@ -356,7 +420,17 @@
         compiler_params=pltpu.CompilerParams(
             collective_id=0, has_side_effects=True, vmem_limit_bytes=56 << 20),
     )(clip_groups, video_clips[0], conv_weight[0], norm_gain, cotangent[0])
-    return (feat[None, None], dweight[None], dgain)
+    feat, dweight, dgain = pl.pallas_call(
+        hand_over,
+        out_shape=(
+            jax.ShapeDtypeStruct((F, C, PIX), BF),
+            jax.ShapeDtypeStruct((6, 1, KK), F32),
+            jax.ShapeDtypeStruct((1, 6), F32),
+        ),
+        in_specs=[vmem, vmem, vmem],
+        out_specs=(vmem, vmem, vmem),
+    )(feat, dweight, dgain)
+    return (feat[None, None], jnp.transpose(dweight, (1, 0, 2)), dgain)
 
 
 def solution(mesh):

time: 77.7 us -> 70.9 us (0.912)
  local copies, waits for them, and re-layouts: 4.6 us -> 0 us
  Pallas kernels: 71.6 us -> 69.4 us
    unnamed x3 -> x0, local copies, waits for them, and re-layouts: 4.6 us -> none
    pallas_call x1, Pallas kernels: 71.6 us -> 67.5 us  [body(): pl.pallas_call(kernel, out_shape=(jax.ShapeDtypeStruct((F, C, PIX), BF),...]
    pallas_call x0 -> x1, Pallas kernels: none -> 1.9 us  [body(): pl.pallas_call(hand_over, out_shape=(jax.ShapeDtypeStruct((F, C, PIX), BF...]
where the time goes in v2:
time: 70.9 us; the launch traced here: 70.7 us
  Pallas kernels  69.4 us (98%)
  between operations  1.29 us (2%)
    pallas_call x1, Pallas kernels, body(): pl.pallas_call(kernel, out_shape=(jax.ShapeDtypeStruct((F, C, PIX), BF),...  67.5 us
    pallas_call x1, Pallas kernels, body(): pl.pallas_call(hand_over, out_shape=(jax.ShapeDtypeStruct((F, C, PIX), BF...  1.9 us

profile of v2, /device:TPU:1, one launch (start us, length us, event | category | flops | bytes accessed | tf_op | source)
XLA Modules:
  0.0 70.7 jit_solution(8095839929450201303)
XLA Ops:
  1.3 67.5 %shard_map.76 = (bf16[9,192,128]{2,1,0:T(8,128)(2,1)}, f32[6,1,5184]{2,1,0:T(1,128)}, f32[1,128]{1,0:T(1,128)}) custom-call(s32[1]{0:T(128)S(6)} %copy.8.groups, bf16[9,192,128]{2,1,0:T(8,128)(2,1)} %bitcast.6, bf16[192,5184]{1,0:T(8,128)(2,1)} %bitcast.5, f32[1,192]{1,0:T(1,128)} %gain.1, bf16[9,192,128]{2,1,0:T(8,128)(2,1)} %bitcast.7), custom_call_target="tpu_custom_call" | custom-call | tf_op jit(solution)/shard_map/pallas_call | solution.py:374
  68.8 1.9 %shard_map.77 = (bf16[9,192,128]{2,1,0:T(8,128)(2,1)}, f32[6,1,5184]{2,1,0:T(1,128)}, f32[1,6]{1,0:T(1,128)}) custom-call(bf16[9,192,128]{2,1,0:T(8,128)(2,1)} %get-tuple-element.9.feat, f32[6,1,5184]{2,1,0:T(1,128)} %get-tuple-element.10.dweight, f32[1,128]{1,0:T(1,128)} %get-tuple-element.11.dgain), custom_call_target="tpu_custom_call" | custom-call | tf_op jit(solution)/shard_map/pallas_call | solution.py:423

commit v3 on v2

v3 whole, which is shorter than its diff:
```python
import jax
import jax.numpy as jnp
from jax import lax
from jax.experimental import pallas as pl
from jax.experimental.pallas import tpu as pltpu
from jax.sharding import PartitionSpec as P

TILE_H = 8
TILE_W = 16
EPS = 1e-06

F = 9
C = 192
PIX = 128
K3 = 9 * C
KK = 27 * C
HK = K3 // 2
N0 = 512
N1 = 384

BF = jnp.bfloat16
F32 = jnp.float32
NT = (((1,), (1,)), ((), ()))


def tap_masks():
    lane = lax.broadcasted_iota(jnp.int32, (1, PIX), 1)
    col = lane & (TILE_W - 1)
    masks = []
    for a in range(3):
        for b in range(3):
            pos = lane + TILE_W * (a - 1)
            ok = (col + (b - 1) >= 0) & (col + (b - 1) < TILE_W) & (pos >= 0) & (pos < PIX)
            masks.append(jnp.where(ok, 1.0, 0.0).astype(BF))
    return masks


def store_patches(dst, base, frame):
    masks = tap_masks()
    values = []
    for a in range(3):
        for b in range(3):
            k = a * 3 + b
            shift = (-(TILE_W * (a - 1) + (b - 1))) % PIX
            values.append(frame if shift == 0 else pltpu.roll(frame, shift, 1) * masks[k])
    patches = jnp.concatenate(values, axis=0)
    dst[pl.ds(base, K3), :] = patches
    return patches


def kernel(groups, video, weight_hbm, gain, cot, feat_hbm, dweight_hbm, dgain_hbm,
           weight, feat, video_v, dweight, dgain, pre, xin, dyin, dysend, fac, scales, gain_b, gain_acc,
           sp, xsp, dp_, wt, dc, odc, acc0, acc1,
           c0, c1, cg, d0, d1, dg, fa0, fa1, fb0, fb1, fg, ga0, ga1, gb0, gb1, gg,
           insem, outsem, featsem, fsend, frecv, bsend, brecv, psend, precv, csend, crecv,
           s1send, s1recv, s2send, s2recv):
    seg = lax.axis_index("segment")
    d = lax.axis_index("dp")
    core = lax.rem(d, 2)
    xc = lax.rem(lax.div(d, 2), 4)
    zc = lax.div(d, 8)

    def dev(z, x, c):
        return {"dp": (z * 4 + x) * 2 + c}

    def put(src, dst, ssem, rsem, where):
        return pltpu.make_async_remote_copy(
            src_ref=src, dst_ref=dst, send_sem=ssem, recv_sem=rsem,
            device_id=where, device_id_type=pl.DeviceIdType.MESH)

    early = pltpu.make_async_copy(weight_hbm.at[:, 2 * K3:], weight.at[:, 2 * K3:], insem.at[0])
    late = pltpu.make_async_copy(weight_hbm.at[:, :2 * K3], weight.at[:, :2 * K3], insem.at[1])
    clip = pltpu.make_async_copy(video, video_v, insem.at[2])
    target = pltpu.make_async_copy(cot, dyin, insem.at[2])

    @pl.when(seg == 0)
    def _():
        clip.start()

    early.start()
    late.start()

    @pl.when(seg == 3)
    def _():
        target.start()

    barrier = pltpu.get_barrier_semaphore()

    def greet(where):
        pl.semaphore_signal(barrier, inc=1, device_id=where, device_id_type=pl.DeviceIdType.MESH)

    greet({"segment": lax.rem(seg + 1, 4)})
    greet({"segment": lax.rem(seg + 3, 4)})
    greet(dev(zc, xc, 1 - core))
    for r in range(1, 4):
        for c in range(2):
            greet(dev(lax.rem(zc + r, 4), xc, c))
            greet(dev(zc, lax.rem(xc + r, 4), c))

    count = groups[0] * 4 - 3

    def keep(i):
        return jnp.where(i < count, 1.0, 0.0).astype(F32)

    zero_patch = jnp.zeros((K3, PIX), BF)
    sp[0:K3, :] = zero_patch
    sp[K3:2 * K3, :] = zero_patch
    sp[11 * K3:, :] = jnp.zeros((32, PIX), BF)
    xsp[0:K3, :] = zero_patch
    xsp[11 * HK:, :] = jnp.zeros((32, PIX), BF)
    dp_[0:K3, :] = zero_patch
    dp_[K3:2 * K3, :] = zero_patch
    pre[...] = jnp.zeros((C, PIX), F32)
    gain_b[...] = jnp.broadcast_to(gain[...], (PIX, C)).T
    gain_acc[...] = jnp.zeros((C, PIX), F32)

    def transpose_weight():
        for tap in range(27):
            to = (tap // 9) * 9 + 8 - tap % 9
            wt[:, to * C:(to + 1) * C] = weight[:, tap * C:(tap + 1) * C].T

    @pl.when(seg == 0)
    def _():
        clip.wait()
        for i in range(F):
            xin[i] = (video_v[i].astype(F32) * keep(i)).astype(BF)

    early.wait()
    late.wait()

    @pl.when(seg >= 2)
    def _():
        transpose_weight()

    def fwd_copy(i):
        return put(feat.at[i], xin.at[i], fsend.at[i], frecv.at[i], {"segment": lax.rem(seg + 1, 4)})

    def bwd_copy(i):
        return put(dysend.at[i], dyin.at[i], bsend.at[i], brecv.at[i], {"segment": lax.rem(seg + 3, 4)})

    def keep_copy(i):
        return pltpu.make_async_copy(feat.at[i], feat_hbm.at[i], featsem.at[i])

    def pair_copy(i):
        src = pl.multiple_of((i + 2) * K3 + HK * (1 - core), 32)
        dst = pl.multiple_of((i + 2) * HK, 32)
        return put(sp.at[pl.ds(src, HK), :], xsp.at[pl.ds(dst, HK), :], psend.at[i], precv.at[i], dev(zc, xc, 1 - core))

    def dconv_copy(i):
        return put(dc.at[i], odc.at[i], csend.at[i], crecv.at[i], dev(zc, xc, 1 - core))

    def forward(i, carry):
        @pl.when(seg > 0)
        def _():
            fwd_copy(i).wait_recv()

        x = xin[i].astype(F32)
        scale = lax.rsqrt(jnp.sum(x * x, axis=0, keepdims=True) * (1.0 / C) + EPS)
        scales[i] = scale
        normed = (x * scale * gain_b[...]).astype(BF)
        patches = store_patches(sp, pl.multiple_of((i + 2) * K3, 64), normed)
        conv = pre[...] + jnp.dot(weight[:, 2 * K3:], patches, preferred_element_type=F32)
        sig = 1.0 / (1.0 + jnp.exp(-conv))
        feat[i] = ((x + conv * sig) * keep(i)).astype(BF)

        @pl.when(i == 0)
        def _():
            pl.semaphore_wait(barrier, 15)

        @pl.when(seg < 3)
        def _():
            fwd_copy(i).start()

        keep_copy(i).start()
        pair_copy(i).start()
        fac[i] = sig * (1.0 + conv * (1.0 - sig))
        window = sp[pl.ds(pl.multiple_of((i + 1) * K3, 64), 2 * K3), :]
        pre[...] = jnp.dot(weight[:, :2 * K3], window, preferred_element_type=F32)
        return carry

    lax.fori_loop(0, F, forward, 0)

    @pl.when(seg < 2)
    def _():
        transpose_weight()

    row = lax.broadcasted_iota(jnp.int32, (C, C), 0)
    colm = lax.broadcasted_iota(jnp.int32, (C, C), 1)
    blk = lax.div(row, 12)
    source = (lax.rem(blk, 4) * 4 + lax.div(blk, 4)) * 12 + lax.rem(row, 12)
    perm = jnp.where(colm == source, 1.0, 0.0).astype(BF)

    def stage1(t, h, r):
        to = lax.rem((zc if h == 0 else xc) + r, 4)
        where = dev(to, xc, core) if h == 0 else dev(zc, to, core)
        src, dst = ((c0, d0), (c1, d1))[h]
        return put(src.at[t, to], dst.at[t, r - 1], s1send.at[t * 2 + h, r - 1], s1recv.at[t * 2 + h, r - 1], where)

    def stage1_gain(r):
        to = lax.rem(zc + r, 4)
        return put(cg.at[to], dg.at[r - 1], s1send.at[6, r - 1], s1recv.at[6, r - 1], dev(to, xc, core))

    def emit(t, part0, part1):
        low = part0.astype(BF)
        high = jnp.dot(perm, part1.astype(BF), preferred_element_type=F32).astype(BF)
        for q in range(4):
            c0[t, q] = low[q * 48:(q + 1) * 48, :]
            c1[t, q] = high[q * 48:(q + 1) * 48, :]
        for r in (2, 1, 3):
            stage1(t, 0, r).start()
            stage1(t, 1, r).start()

    def emit_gain():
        low = gain_acc[...].astype(BF)
        for q in range(4):
            cg[q] = low[q * 48:(q + 1) * 48, :]
        for r in (2, 1, 3):
            stage1_gain(r).start()

    def patch_rows(t, i, start, size):
        own = pl.multiple_of((i + t) * K3 + HK * core + start, 32)
        other = pl.multiple_of((i + t) * HK + start, 32)
        return [sp[pl.ds(own, size), :], xsp[pl.ds(other, size), :]]

    def weight_product(t, frames, start, size):
        lhs, rhs = [], []
        for i in frames:
            lhs += [dc[i], odc[i]]
            rhs += patch_rows(t, i, start, size)
        return lax.dot_general(jnp.concatenate(lhs, axis=1), jnp.concatenate(rhs, axis=1), NT,
                               preferred_element_type=F32)

    pre[...] = jnp.zeros((C, PIX), F32)

    def wait_pairs():
        def body_(i, carry):
            pair_copy(i).wait_recv()
            return carry
        lax.fori_loop(0, F, body_, 0)

    @pl.when(seg == 3)
    def _():
        target.wait()

    def backward(n, carry):
        i = F - 1 - n

        @pl.when(seg < 3)
        def _():
            bwd_copy(i).wait_recv()

        dz = dyin[i].astype(F32) * keep(i)
        dconv = (dz * fac[i]).astype(BF)
        dc[i] = dconv
        patches = store_patches(dp_, pl.multiple_of((n + 2) * K3, 64), dconv)
        dnormed = pre[...] + jnp.dot(wt[:, 2 * K3:], patches, preferred_element_type=F32)
        x = xin[i].astype(F32)
        scale = scales[i]
        gx = dnormed * gain_b[...]
        inner = jnp.sum(gx * x, axis=0, keepdims=True)
        dx = scale * gx - x * (scale * scale * scale * inner * (1.0 / C)) + dz
        dysend[i] = dx.astype(BF)
        bwd_copy(i).start()
        dconv_copy(i).start()
        gain_acc[...] += dnormed * x * scale
        window = dp_[pl.ds(pl.multiple_of((n + 1) * K3, 64), 2 * K3), :]
        pre[...] = jnp.dot(wt[:, :2 * K3], window, preferred_element_type=F32)
        return carry

    @pl.when(seg > 0)
    def _():
        lax.fori_loop(0, F, backward, 0)
        emit_gain()
        wait_pairs()

        def arrived(i, carry):
            dconv_copy(i).wait_recv()
            return carry

        lax.fori_loop(0, F, arrived, 0)
        for t in range(3):
            frames = range(2 - t, F)
            emit(t, weight_product(t, frames, 0, N0), weight_product(t, frames, N0, N1))

    def take(n):
        i = F - 1 - n
        bwd_copy(i).wait_recv()
        dconv = (dyin[i].astype(F32) * keep(i) * fac[i]).astype(BF)
        dc[i] = dconv
        dconv_copy(i).start()
        store_patches(dp_, pl.multiple_of((n + 2) * K3, 64), dconv)

    def accumulate(t, i):
        acc0[t] += weight_product(t, [i], 0, N0)
        acc1[t] += weight_product(t, [i], N0, N1)

    @pl.when(seg == 0)
    def _():
        wait_pairs()
        acc0[...] = jnp.zeros((3, C, N0), F32)
        acc1[...] = jnp.zeros((3, C, N1), F32)
        take(0)

        def step(n, carry):
            take(n)
            i = F - n
            dconv_copy(i).wait_recv()
            for t in range(3):
                accumulate(t, i)
            return carry

        lax.fori_loop(1, F - 1, step, 0)
        emit(0, acc0[0], acc1[0])
        take(F - 1)
        dconv_copy(1).wait_recv()
        accumulate(1, 1)
        emit(1, acc0[1], acc1[1])
        accumulate(2, 1)
        dconv_copy(0).wait_recv()
        accumulate(2, 0)
        emit(2, acc0[2], acc1[2])

        def add_gain(n, dnormed):
            i = F - 1 - n
            gain_acc[...] += dnormed * xin[i].astype(F32) * scales[i]

        def two(j, carry):
            n = j * 2
            first = dp_[pl.ds(pl.multiple_of(n * K3, 64), KK), :]
            second = dp_[pl.ds(pl.multiple_of((n + 1) * K3, 64), KK), :]
            both = jnp.dot(wt[...], jnp.concatenate([first, second], axis=1), preferred_element_type=F32)
            add_gain(n, both[:, :PIX])
            add_gain(n + 1, both[:, PIX:])
            return carry

        lax.fori_loop(0, 4, two, 0)
        add_gain(8, jnp.dot(wt[...], dp_[8 * K3:8 * K3 + KK, :], preferred_element_type=F32))
        emit_gain()

    prow = lax.broadcasted_iota(jnp.int32, (64, 48), 0)
    pcol = lax.broadcasted_iota(jnp.int32, (64, 48), 1)
    spread = jnp.where((lax.rem(prow, 8) < 6) & (pcol == lax.div(prow, 8) * 6 + lax.rem(prow, 8)), 1.0, 0.0).astype(BF)

    batches = ((0, 0, fa0, ga0), (1, 1, fa1, ga1), (2, 0, fb0, gb0), (3, 1, fb1, gb1), (4, 0, fg, gg))

    def stage2(batch, r, c):
        k, h, src, dst = batch
        if h == 0:
            to = lax.rem(xc + r, 4)
            where = dev(zc, to, c)
        else:
            to = lax.rem(zc + r, 4)
            where = dev(to, xc, c)
        slot = r * 2 + jnp.where(c == core, 0, 1)
        return put(src.at[to * 2 + c], dst.at[core * 4 + r], s2send.at[k, slot], s2recv.at[k, slot], where)

    def send_batch(batch):
        for r in (2, 1, 3):
            stage2(batch, r, core).start()
            stage2(batch, r, 1 - core).start()
        stage2(batch, 0, 1 - core).start()

    def collect(own, got, out, part):
        total = own.astype(F32)
        for r in range(3):
            total = total + got[r].astype(F32)
        spaced = jnp.dot(spread, total.astype(BF), preferred_element_type=F32).astype(BF)
        for k in range(8):
            out[k, part] = spaced[k * 8:(k + 1) * 8, :]

    def finish_stage1(t, h):
        for r in range(1, 4):
            stage1(t, h, r).wait_recv()
        own, got = ((c0, d0), (c1, d1))[h]
        out = ((fa0, fa1), (fa0, fa1), (fb0, fb1))[t][h]
        collect(own[t, zc if h == 0 else xc], got[t], out, t % 2)

    for h in range(2):
        finish_stage1(0, h)
        finish_stage1(1, h)
        send_batch(batches[h])
    for h in range(2):
        finish_stage1(2, h)
        send_batch(batches[2 + h])
    for r in range(1, 4):
        stage1_gain(r).wait_recv()
    collect(cg[zc], dg[...], fg, 0)
    send_batch(batches[4])

    def stage2_wait(batch, r, c):
        k, h, src, dst = batch
        slot = r * 2 + jnp.where(c == core, 0, 1)
        where = dev(zc, lax.rem(xc + r, 4), c) if h == 0 else dev(lax.rem(zc + r, 4), xc, c)
        return put(src.at[0], dst.at[c * 4 + r], s2send.at[k, slot], s2recv.at[k, slot], where)

    for batch in batches:
        k, h, src, dst = batch
        mine = (xc if h == 0 else zc) * 2 + core
        dst[core * 4] = src[mine]
        for r in range(4):
            if r:
                stage2_wait(batch, r, core).wait_recv()
            stage2_wait(batch, r, 1 - core).wait_recv()
        if k == 4:
            total = dst[0, 0].astype(F32)
            for q in range(1, 8):
                total = total + dst[q, 0].astype(F32)
            per_row = jnp.sum(total, axis=1, keepdims=True)
            r8 = lax.broadcasted_iota(jnp.int32, (8, 128), 0)
            l8 = lax.broadcasted_iota(jnp.int32, (8, 128), 1)
            dgain[...] = jnp.sum(jnp.where(r8 == l8, per_row, 0.0), axis=0, keepdims=True)
            continue
        for part in range(2 if k < 2 else 1):
            t = part if k < 2 else 2
            for c in range(2):
                total = dst[c * 4, part].astype(F32)
                for r in range(1, 4):
                    total = total + dst[c * 4 + r, part].astype(F32)
                start = t * K3 + c * HK + (0 if h == 0 else N0)
                size = N0 if h == 0 else HK - N0
                for j in range(6):
                    dweight[j, :, start:start + size] = total[j:j + 1, 0:size]

    results = (pltpu.make_async_copy(dweight, dweight_hbm, outsem.at[0]),
               pltpu.make_async_copy(dgain, dgain_hbm, outsem.at[1]))
    for result in results:
        result.start()

    def settle(i, carry):
        keep_copy(i).wait()
        pair_copy(i).wait_send()
        dconv_copy(i).wait_send()

        @pl.when(seg < 3)
        def _():
            fwd_copy(i).wait_send()

        @pl.when(seg > 0)
        def _():
            bwd_copy(i).wait_send()

        return carry

    lax.fori_loop(0, F, settle, 0)
    for r in range(1, 4):
        for t in range(3):
            stage1(t, 0, r).wait_send()
            stage1(t, 1, r).wait_send()
        stage1_gain(r).wait_send()
    for batch in batches:
        for r in range(4):
            if r:
                stage2_wait(batch, r, core).wait_send()
            stage2_wait(batch, r, 1 - core).wait_send()
    for result in results:
        result.wait()


def hand_over(feat, dweight, dgain, feat_out, dweight_out, dgain_out):
    feat_out[...] = feat[...]
    dweight_out[...] = dweight[...]
    dgain_out[...] = dgain[:, 0:6]


def body(video_clips, conv_weight, norm_gain, cotangent, clip_groups):
    vmem = pl.BlockSpec(memory_space=pltpu.VMEM)
    hbm = pl.BlockSpec(memory_space=pl.ANY)
    smem = pl.BlockSpec(memory_space=pltpu.SMEM)
    dma = pltpu.SemaphoreType.DMA
    feat, dweight, dgain = pl.pallas_call(
        kernel,
        out_shape=(
            jax.ShapeDtypeStruct((F, C, PIX), BF),
            jax.ShapeDtypeStruct((6, 1, KK), F32),
            jax.ShapeDtypeStruct((1, 128), F32),
        ),
        in_specs=[smem, hbm, hbm, vmem, hbm],
        out_specs=(hbm, hbm, hbm),
        scratch_shapes=[
            pltpu.VMEM((C, KK), BF),
            pltpu.VMEM((F, C, PIX), BF),
            pltpu.VMEM((F, C, PIX), BF),
            pltpu.VMEM((6, 1, KK), F32),
            pltpu.VMEM((1, 128), F32),
            pltpu.VMEM((C, PIX), F32),
            pltpu.VMEM((F, C, PIX), BF),
            pltpu.VMEM((F, C, PIX), BF),
            pltpu.VMEM((F, C, PIX), BF),
            pltpu.VMEM((F, C, PIX), F32),
            pltpu.VMEM((F, 1, PIX), F32),
            pltpu.VMEM((C, PIX), F32),
            pltpu.VMEM((C, PIX), F32),
            pltpu.VMEM((11 * K3 + 32, PIX), BF),
            pltpu.VMEM((11 * HK + 32, PIX), BF),
            pltpu.VMEM((11 * K3, PIX), BF),
            pltpu.VMEM((C, KK), BF),
            pltpu.VMEM((F, C, PIX), BF),
            pltpu.VMEM((F, C, PIX), BF),
            pltpu.VMEM((3, C, N0), F32),
            pltpu.VMEM((3, C, N1), F32),
            pltpu.VMEM((3, 4, 48, N0), BF),
            pltpu.VMEM((3, 4, 48, N1), BF),
            pltpu.VMEM((4, 48, PIX), BF),
            pltpu.VMEM((3, 3, 48, N0), BF),
            pltpu.VMEM((3, 3, 48, N1), BF),
            pltpu.VMEM((3, 48, PIX), BF),
            pltpu.VMEM((8, 2, 8, N0), BF),
            pltpu.VMEM((8, 2, 8, N1), BF),
            pltpu.VMEM((8, 1, 8, N0), BF),
            pltpu.VMEM((8, 1, 8, N1), BF),
            pltpu.VMEM((8, 1, 8, PIX), BF),
            pltpu.VMEM((8, 2, 8, N0), BF),
            pltpu.VMEM((8, 2, 8, N1), BF),
            pltpu.VMEM((8, 1, 8, N0), BF),
            pltpu.VMEM((8, 1, 8, N1), BF),
            pltpu.VMEM((8, 1, 8, PIX), BF),
            dma((3,)), dma((2,)), dma((F,)),
            dma((F,)), dma((F,)), dma((F,)), dma((F,)),
            dma((F,)), dma((F,)), dma((F,)), dma((F,)),
            dma((7, 3)), dma((7, 3)),
            dma((5, 8)), dma((5, 8)),
        ],
        compiler_params=pltpu.CompilerParams(
            collective_id=0, has_side_effects=True, vmem_limit_bytes=56 << 20),
    )(clip_groups, video_clips[0], conv_weight[0], norm_gain, cotangent[0])
    feat, dweight, dgain = pl.pallas_call(
        hand_over,
        out_shape=(
            jax.ShapeDtypeStruct((F, C, PIX), BF),
            jax.ShapeDtypeStruct((6, 1, KK), F32),
            jax.ShapeDtypeStruct((1, 6), F32),
        ),
        in_specs=[vmem, vmem, vmem],
        out_specs=(vmem, vmem, vmem),
    )(feat, dweight, dgain)
    return (feat[None, None], jnp.transpose(dweight, (1, 0, 2)), dgain)


def solution(mesh):
    placed = (
        P("dp", None, None, None),
        P("segment", None, None),
        P("segment", None),
        P("dp", None, None, None),
        P("dp"),
    )
    return jax.shard_map(
        body,
        mesh=mesh,
        in_specs=placed,
        out_specs=(
            P("segment", "dp", None, None, None),
            P("segment", "dp", None),
            P("segment", "dp"),
        ),
        check_vma=False,
    )
```

time: 70.9 us -> 67.7 us (0.955)
  Pallas kernels: 69.4 us -> 66.3 us
    pallas_call x1, Pallas kernels: 67.5 us -> 64.4 us  [body(): pl.pallas_call(kernel, out_shape=(jax.ShapeDtypeStruct((F, C, PIX), BF),...]
where the time goes in v3:
time: 67.7 us; the launch traced here: 67.6 us
  Pallas kernels  66.3 us (98%)
  between operations  1.29 us (2%)
    pallas_call x1, Pallas kernels, body(): pl.pallas_call(kernel, out_shape=(jax.ShapeDtypeStruct((F, C, PIX), BF),...  64.4 us
    pallas_call x1, Pallas kernels, body(): pl.pallas_call(hand_over, out_shape=(jax.ShapeDtypeStruct((F, C, PIX), BF...  1.9 us

profile of v3, /device:TPU:1, one launch (start us, length us, event | category | flops | bytes accessed | tf_op | source)
XLA Modules:
  0.0 67.6 jit_solution(10474717705668147062)
XLA Ops:
  1.3 64.4 %shard_map.76 = (bf16[9,192,128]{2,1,0:T(8,128)(2,1)}, f32[6,1,5184]{2,1,0:T(1,128)}, f32[1,128]{1,0:T(1,128)}) custom-call(s32[1]{0:T(128)S(6)} %copy.8.groups, bf16[9,192,128]{2,1,0:T(8,128)(2,1)} %bitcast.6, bf16[192,5184]{1,0:T(8,128)(2,1)} %bitcast.5, f32[1,192]{1,0:T(1,128)} %gain.1, bf16[9,192,128]{2,1,0:T(8,128)(2,1)} %bitcast.7), custom_call_target="tpu_custom_call" | custom-call | tf_op jit(solution)/shard_map/pallas_call | solution.py:470
  65.7 1.9 %shard_map.77 = (bf16[9,192,128]{2,1,0:T(8,128)(2,1)}, f32[6,1,5184]{2,1,0:T(1,128)}, f32[1,6]{1,0:T(1,128)}) custom-call(bf16[9,192,128]{2,1,0:T(8,128)(2,1)} %get-tuple-element.9.feat, f32[6,1,5184]{2,1,0:T(1,128)} %get-tuple-element.10.dweight, f32[1,128]{1,0:T(1,128)} %get-tuple-element.11.dgain), custom_call_target="tpu_custom_call" | custom-call | tf_op jit(solution)/shard_map/pallas_call | solution.py:526

commit v4 on v3

--- a/solution.py
+++ b/solution.py
@@ -50,8 +50,8 @@
 
 def kernel(groups, video, weight_hbm, gain, cot, feat_hbm, dweight_hbm, dgain_hbm,
            weight, feat, video_v, dweight, dgain, pre, xin, dyin, dysend, fac, scales, gain_b, gain_acc,
-           sp, xsp, dp_, wt, dc, odc, acc0, acc1,
-           c0, c1, cg, d0, d1, dg, fa0, fa1, fb0, fb1, fg, ga0, ga1, gb0, gb1, gg,
+           sp, xsp, dp_, wt, whalf, fold, dc, odc, acc0, acc1, col_sum,
+           c0, c1, cg, d0, d1, dg, f0, f1, g0, g1,
            insem, outsem, featsem, fsend, frecv, bsend, brecv, psend, precv, csend, crecv,
            s1send, s1recv, s2send, s2recv):
     seg = lax.axis_index("segment")
@@ -97,7 +97,7 @@
             greet(dev(lax.rem(zc + r, 4), xc, c))
             greet(dev(zc, lax.rem(xc + r, 4), c))
 
-    count = groups[0] * 4 - 3
+    count = groups[...] * 4 - 3
 
     def keep(i):
         return jnp.where(i < count, 1.0, 0.0).astype(F32)
@@ -113,11 +113,27 @@
     pre[...] = jnp.zeros((C, PIX), F32)
     gain_b[...] = jnp.broadcast_to(gain[...], (PIX, C)).T
     gain_acc[...] = jnp.zeros((C, PIX), F32)
+    col_sum[...] = jnp.zeros((8, N0 + N1), F32)
+    acc0[...] = jnp.zeros((3, C, N0), F32)
+    acc1[...] = jnp.zeros((3, C, N1), F32)
 
     def transpose_weight():
         for tap in range(27):
             to = (tap // 9) * 9 + 8 - tap % 9
             wt[:, to * C:(to + 1) * C] = weight[:, tap * C:(tap + 1) * C].T
+
+    def own_weight():
+        for t in range(3):
+            for c in range(2):
+                @pl.when(core == c)
+                def _():
+                    start = t * K3 + c * HK
+                    whalf[t, :, 0:HK] = weight[:, start:start + HK]
+
+            whalf[t, :, HK:] = jnp.zeros((C, N0 + N1 - HK), BF)
+        lane = lax.broadcasted_iota(jnp.int32, (C, N0 + N1), 1) + HK * core
+        channel = lax.broadcasted_iota(jnp.int32, (C, N0 + N1), 0)
+        fold[...] = jnp.where(lax.rem(lane, C) == channel, 1.0, 0.0).astype(BF)
 
     @pl.when(seg == 0)
     def _():
@@ -180,42 +196,66 @@
 
     lax.fori_loop(0, F, forward, 0)
 
-    @pl.when(seg < 2)
+    @pl.when(seg == 1)
     def _():
         transpose_weight()
+
+    @pl.when(seg == 0)
+    def _():
+        own_weight()
 
     row = lax.broadcasted_iota(jnp.int32, (C, C), 0)
     colm = lax.broadcasted_iota(jnp.int32, (C, C), 1)
     blk = lax.div(row, 12)
-    source = (lax.rem(blk, 4) * 4 + lax.div(blk, 4)) * 12 + lax.rem(row, 12)
-    perm = jnp.where(colm == source, 1.0, 0.0).astype(BF)
+    swapped = (lax.rem(blk, 4) * 4 + lax.div(blk, 4)) * 12 + lax.rem(row, 12)
+
+    def z_first(h):
+        return 1 - lax.rem(core + h, 2)
+
+    def pick(h, first, second):
+        return first * z_first(h) + second * (1 - z_first(h))
+
+    def order(h):
+        return jnp.where(colm == pick(h, row, swapped), 1.0, 0.0).astype(BF)
 
     def stage1(t, h, r):
-        to = lax.rem((zc if h == 0 else xc) + r, 4)
-        where = dev(to, xc, core) if h == 0 else dev(zc, to, core)
-        src, dst = ((c0, d0), (c1, d1))[h]
-        return put(src.at[t, to], dst.at[t, r - 1], s1send.at[t * 2 + h, r - 1], s1recv.at[t * 2 + h, r - 1], where)
-
-    def stage1_gain(r):
-        to = lax.rem(zc + r, 4)
-        return put(cg.at[to], dg.at[r - 1], s1send.at[6, r - 1], s1recv.at[6, r - 1], dev(to, xc, core))
-
-    def emit(t, part0, part1):
-        low = part0.astype(BF)
-        high = jnp.dot(perm, part1.astype(BF), preferred_element_type=F32).astype(BF)
+        to = lax.rem(pick(h, zc, xc) + r, 4)
+        where = {"dp": pick(h, to * 8 + xc * 2, zc * 8 + to * 2) + core}
+        if h == 1:
+            src, dst = c1.at[t, to], d1.at[t, r - 1]
+        elif t < 2:
+            src, dst = c0.at[t, to], d0.at[t, r - 1]
+        else:
+            src, dst = cg.at[to], dg.at[r - 1]
+        return put(src, dst, s1send.at[t * 2 + h, r - 1], s1recv.at[t * 2 + h, r - 1], where)
+
+    def emit(t, h, part):
+        value = part.astype(BF)
+        if t == 2 and h == 0:
+            value = jnp.concatenate([value, gain_acc[...].astype(BF)], axis=1)
+        rows = jnp.dot(order(h), value, preferred_element_type=F32).astype(BF)
         for q in range(4):
-            c0[t, q] = low[q * 48:(q + 1) * 48, :]
-            c1[t, q] = high[q * 48:(q + 1) * 48, :]
+            if h == 1:
+                c1[t, q] = rows[q * 48:(q + 1) * 48, :]
+            elif t < 2:
+                c0[t, q] = rows[q * 48:(q + 1) * 48, :]
+            else:
+                cg[q] = rows[q * 48:(q + 1) * 48, :]
         for r in (2, 1, 3):
-            stage1(t, 0, r).start()
-            stage1(t, 1, r).start()
-
-    def emit_gain():
-        low = gain_acc[...].astype(BF)
-        for q in range(4):
-            cg[q] = low[q * 48:(q + 1) * 48, :]
-        for r in (2, 1, 3):
-            stage1_gain(r).start()
+            stage1(t, h, r).start()
+
+    def add_columns(t):
+        for acc, start, size in ((acc0, 0, N0), (acc1, N0, N1)):
+            product = acc[t] * whalf[t, :, start:start + size].astype(F32)
+            col_sum[:, start:start + size] += jnp.sum(product.reshape(C // 8, 8, size), axis=0)
+
+    def gain_from_columns():
+        sums = col_sum[...]
+        high = sums.astype(BF)
+        low = (sums - high.astype(F32)).astype(BF)
+        both = jnp.concatenate([high, low], axis=0)
+        per_channel = lax.dot_general(fold[...], both, NT, preferred_element_type=F32)
+        gain_acc[:, 0:16] = per_channel / gain_b[:, 0:16]
 
     def patch_rows(t, i, start, size):
         own = pl.multiple_of((i + t) * K3 + HK * core + start, 32)
@@ -241,6 +281,10 @@
     @pl.when(seg == 3)
     def _():
         target.wait()
+
+    def accumulate(t, i):
+        acc0[t] += weight_product(t, [i], 0, N0)
+        acc1[t] += weight_product(t, [i], N0, N1)
 
     def backward(n, carry):
         i = F - 1 - n
@@ -262,15 +306,15 @@
         dysend[i] = dx.astype(BF)
         bwd_copy(i).start()
         dconv_copy(i).start()
-        gain_acc[...] += dnormed * x * scale
         window = dp_[pl.ds(pl.multiple_of((n + 1) * K3, 64), 2 * K3), :]
         pre[...] = jnp.dot(wt[:, :2 * K3], window, preferred_element_type=F32)
+
+        gain_acc[...] += dnormed * x * scale
         return carry
 
     @pl.when(seg > 0)
     def _():
         lax.fori_loop(0, F, backward, 0)
-        emit_gain()
         wait_pairs()
 
         def arrived(i, carry):
@@ -280,7 +324,8 @@
         lax.fori_loop(0, F, arrived, 0)
         for t in range(3):
             frames = range(2 - t, F)
-            emit(t, weight_product(t, frames, 0, N0), weight_product(t, frames, N0, N1))
+            emit(t, 0, weight_product(t, frames, 0, N0))
+            emit(t, 1, weight_product(t, frames, N0, N1))
 
     def take(n):
         i = F - 1 - n
@@ -288,17 +333,10 @@
         dconv = (dyin[i].astype(F32) * keep(i) * fac[i]).astype(BF)
         dc[i] = dconv
         dconv_copy(i).start()
-        store_patches(dp_, pl.multiple_of((n + 2) * K3, 64), dconv)
-
-    def accumulate(t, i):
-        acc0[t] += weight_product(t, [i], 0, N0)
-        acc1[t] += weight_product(t, [i], N0, N1)
 
     @pl.when(seg == 0)
     def _():
         wait_pairs()
-        acc0[...] = jnp.zeros((3, C, N0), F32)
-        acc1[...] = jnp.zeros((3, C, N1), F32)
         take(0)
 
         def step(n, carry):
@@ -310,148 +348,124 @@
             return carry
 
         lax.fori_loop(1, F - 1, step, 0)
-        emit(0, acc0[0], acc1[0])
+        emit(0, 0, acc0[0])
+        emit(0, 1, acc1[0])
         take(F - 1)
         dconv_copy(1).wait_recv()
         accumulate(1, 1)
-        emit(1, acc0[1], acc1[1])
+        emit(1, 0, acc0[1])
+        emit(1, 1, acc1[1])
         accumulate(2, 1)
+        for t in range(2):
+            add_columns(t)
         dconv_copy(0).wait_recv()
         accumulate(2, 0)
-        emit(2, acc0[2], acc1[2])
-
-        def add_gain(n, dnormed):
-            i = F - 1 - n
-            gain_acc[...] += dnormed * xin[i].astype(F32) * scales[i]
-
-        def two(j, carry):
-            n = j * 2
-            first = dp_[pl.ds(pl.multiple_of(n * K3, 64), KK), :]
-            second = dp_[pl.ds(pl.multiple_of((n + 1) * K3, 64), KK), :]
-            both = jnp.dot(wt[...], jnp.concatenate([first, second], axis=1), preferred_element_type=F32)
-            add_gain(n, both[:, :PIX])
-            add_gain(n + 1, both[:, PIX:])
-            return carry
-
-        lax.fori_loop(0, 4, two, 0)
-        add_gain(8, jnp.dot(wt[...], dp_[8 * K3:8 * K3 + KK, :], preferred_element_type=F32))
-        emit_gain()
+        emit(2, 1, acc1[2])
+        add_columns(2)
+        gain_from_columns()
+        emit(2, 0, acc0[2])
 
     prow = lax.broadcasted_iota(jnp.int32, (64, 48), 0)
     pcol = lax.broadcasted_iota(jnp.int32, (64, 48), 1)
     spread = jnp.where((lax.rem(prow, 8) < 6) & (pcol == lax.div(prow, 8) * 6 + lax.rem(prow, 8)), 1.0, 0.0).astype(BF)
 
-    batches = ((0, 0, fa0, ga0), (1, 1, fa1, ga1), (2, 0, fb0, gb0), (3, 1, fb1, gb1), (4, 0, fg, gg))
-
-    def stage2(batch, r, c):
-        k, h, src, dst = batch
-        if h == 0:
-            to = lax.rem(xc + r, 4)
-            where = dev(zc, to, c)
-        else:
-            to = lax.rem(zc + r, 4)
-            where = dev(to, xc, c)
+    def stage2(h, r, c):
+        to = lax.rem(pick(h, xc, zc) + r, 4)
+        where = {"dp": pick(h, zc * 8 + to * 2, to * 8 + xc * 2) + c}
         slot = r * 2 + jnp.where(c == core, 0, 1)
-        return put(src.at[to * 2 + c], dst.at[core * 4 + r], s2send.at[k, slot], s2recv.at[k, slot], where)
-
-    def send_batch(batch):
-        for r in (2, 1, 3):
-            stage2(batch, r, core).start()
-            stage2(batch, r, 1 - core).start()
-        stage2(batch, 0, 1 - core).start()
-
-    def collect(own, got, out, part):
+        src, dst = ((f0, g0), (f1, g1))[h]
+        return put(src.at[to * 2 + c], dst.at[core * 4 + r], s2send.at[h, slot], s2recv.at[h, slot], where)
+
+    def collect(own, got, out, start, size):
         total = own.astype(F32)
         for r in range(3):
             total = total + got[r].astype(F32)
         spaced = jnp.dot(spread, total.astype(BF), preferred_element_type=F32).astype(BF)
         for k in range(8):
-            out[k, part] = spaced[k * 8:(k + 1) * 8, :]
+            out[k, :, start:start + size] = spaced[k * 8:(k + 1) * 8, :]
 
     def finish_stage1(t, h):
         for r in range(1, 4):
             stage1(t, h, r).wait_recv()
-        own, got = ((c0, d0), (c1, d1))[h]
-        out = ((fa0, fa1), (fa0, fa1), (fb0, fb1))[t][h]
-        collect(own[t, zc if h == 0 else xc], got[t], out, t % 2)
-
-    for h in range(2):
-        finish_stage1(0, h)
-        finish_stage1(1, h)
-        send_batch(batches[h])
-    for h in range(2):
+        me = pick(h, zc, xc)
+        if h == 1:
+            collect(c1[t, me], d1[t], f1, t * N1, N1)
+        elif t < 2:
+            collect(c0[t, me], d0[t], f0, t * N0, N0)
+        else:
+            collect(cg[me], dg[...], f0, 2 * N0, N0 + PIX)
+
+    def settle(i, carry):
+        keep_copy(i).wait()
+        pair_copy(i).wait_send()
+        dconv_copy(i).wait_send()
+
+        @pl.when(seg < 3)
+        def _():
+            fwd_copy(i).wait_send()
+
+        @pl.when(seg > 0)
+        def _():
+            bwd_copy(i).wait_send()
+
+        return carry
+
+    for t in range(2):
+        for h in range(2):
+            finish_stage1(t, h)
+    lax.fori_loop(0, F, settle, 0)
+    for h in (1, 0):
         finish_stage1(2, h)
-        send_batch(batches[2 + h])
+        for r in (2, 1, 3):
+            stage2(h, r, core).start()
+            stage2(h, r, 1 - core).start()
+        stage2(h, 0, 1 - core).start()
+
     for r in range(1, 4):
-        stage1_gain(r).wait_recv()
-    collect(cg[zc], dg[...], fg, 0)
-    send_batch(batches[4])
-
-    def stage2_wait(batch, r, c):
-        k, h, src, dst = batch
+        for t in range(3):
+            stage1(t, 0, r).wait_send()
+            stage1(t, 1, r).wait_send()
+
+    def stage2_wait(h, r, c):
         slot = r * 2 + jnp.where(c == core, 0, 1)
-        where = dev(zc, lax.rem(xc + r, 4), c) if h == 0 else dev(lax.rem(zc + r, 4), xc, c)
-        return put(src.at[0], dst.at[c * 4 + r], s2send.at[k, slot], s2recv.at[k, slot], where)
-
-    for batch in batches:
-        k, h, src, dst = batch
-        mine = (xc if h == 0 else zc) * 2 + core
-        dst[core * 4] = src[mine]
+        src, dst = ((f0, g0), (f1, g1))[h]
+        return put(src.at[0], dst.at[c * 4 + r], s2send.at[h, slot], s2recv.at[h, slot], dev(zc, xc, 1 - core))
+
+    for h in (1, 0):
+        src, dst = ((f0, g0), (f1, g1))[h]
+        dst[core * 4] = src[pick(h, xc, zc) * 2 + core]
         for r in range(4):
             if r:
-                stage2_wait(batch, r, core).wait_recv()
-            stage2_wait(batch, r, 1 - core).wait_recv()
-        if k == 4:
-            total = dst[0, 0].astype(F32)
-            for q in range(1, 8):
-                total = total + dst[q, 0].astype(F32)
-            per_row = jnp.sum(total, axis=1, keepdims=True)
-            r8 = lax.broadcasted_iota(jnp.int32, (8, 128), 0)
-            l8 = lax.broadcasted_iota(jnp.int32, (8, 128), 1)
-            dgain[...] = jnp.sum(jnp.where(r8 == l8, per_row, 0.0), axis=0, keepdims=True)
-            continue
-        for part in range(2 if k < 2 else 1):
-            t = part if k < 2 else 2
-            for c in range(2):
-                total = dst[c * 4, part].astype(F32)
-                for r in range(1, 4):
-                    total = total + dst[c * 4 + r, part].astype(F32)
+                stage2_wait(h, r, core).wait_recv()
+            stage2_wait(h, r, 1 - core).wait_recv()
+        for c in range(2):
+            total = dst[c * 4].astype(F32)
+            for r in range(1, 4):
+                total = total + dst[c * 4 + r].astype(F32)
+            if h == 0:
+                per_row = jnp.sum(total[:, 3 * N0:], axis=1, keepdims=True)
+                gain_rows = per_row if c == 0 else gain_rows + per_row
+            for t in range(3):
                 start = t * K3 + c * HK + (0 if h == 0 else N0)
                 size = N0 if h == 0 else HK - N0
+                first = t * (N0 if h == 0 else N1)
                 for j in range(6):
-                    dweight[j, :, start:start + size] = total[j:j + 1, 0:size]
+                    dweight[j, :, start:start + size] = total[j:j + 1, first:first + size]
+
+    r8 = lax.broadcasted_iota(jnp.int32, (8, 128), 0)
+    l8 = lax.broadcasted_iota(jnp.int32, (8, 128), 1)
+    dgain[...] = jnp.sum(jnp.where(r8 == l8, gain_rows, 0.0), axis=0, keepdims=True)
 
     results = (pltpu.make_async_copy(dweight, dweight_hbm, outsem.at[0]),
                pltpu.make_async_copy(dgain, dgain_hbm, outsem.at[1]))
     for result in results:
         result.start()
 
-    def settle(i, carry):
-        keep_copy(i).wait()
-        pair_copy(i).wait_send()
-        dconv_copy(i).wait_send()
-
-        @pl.when(seg < 3)
-        def _():
-            fwd_copy(i).wait_send()
-
-        @pl.when(seg > 0)
-        def _():
-            bwd_copy(i).wait_send()
-
-        return carry
-
-    lax.fori_loop(0, F, settle, 0)
-    for r in range(1, 4):
-        for t in range(3):
-            stage1(t, 0, r).wait_send()
-            stage1(t, 1, r).wait_send()
-        stage1_gain(r).wait_send()
-    for batch in batches:
+    for h in range(2):
         for r in range(4):
             if r:
-                stage2_wait(batch, r, core).wait_send()
-            stage2_wait(batch, r, 1 - core).wait_send()
+                stage2_wait(h, r, core).wait_send()
+            stage2_wait(h, r, 1 - core).wait_send()
     for result in results:
         result.wait()
 
@@ -465,7 +479,6 @@
 def body(video_clips, conv_weight, norm_gain, cotangent, clip_groups):
     vmem = pl.BlockSpec(memory_space=pltpu.VMEM)
     hbm = pl.BlockSpec(memory_space=pl.ANY)
-    smem = pl.BlockSpec(memory_space=pltpu.SMEM)
     dma = pltpu.SemaphoreType.DMA
     feat, dweight, dgain = pl.pallas_call(
         kernel,
@@ -474,7 +487,7 @@
             jax.ShapeDtypeStruct((6, 1, KK), F32),
             jax.ShapeDtypeStruct((1, 128), F32),
         ),
-        in_specs=[smem, hbm, hbm, vmem, hbm],
+        in_specs=[vmem, hbm, hbm, vmem, hbm],
         out_specs=(hbm, hbm, hbm),
         scratch_shapes=[
             pltpu.VMEM((C, KK), BF),
@@ -494,35 +507,32 @@
             pltpu.VMEM((11 * HK + 32, PIX), BF),
             pltpu.VMEM((11 * K3, PIX), BF),
             pltpu.VMEM((C, KK), BF),
+            pltpu.VMEM((3, C, N0 + N1), BF),
+            pltpu.VMEM((C, N0 + N1), BF),
             pltpu.VMEM((F, C, PIX), BF),
             pltpu.VMEM((F, C, PIX), BF),
             pltpu.VMEM((3, C, N0), F32),
             pltpu.VMEM((3, C, N1), F32),
-            pltpu.VMEM((3, 4, 48, N0), BF),
+            pltpu.VMEM((8, N0 + N1), F32),
+            pltpu.VMEM((2, 4, 48, N0), BF),
             pltpu.VMEM((3, 4, 48, N1), BF),
-            pltpu.VMEM((4, 48, PIX), BF),
-            pltpu.VMEM((3, 3, 48, N0), BF),
+            pltpu.VMEM((4, 48, N0 + PIX), BF),
+            pltpu.VMEM((2, 3, 48, N0), BF),
             pltpu.VMEM((3, 3, 48, N1), BF),
-            pltpu.VMEM((3, 48, PIX), BF),
-            pltpu.VMEM((8, 2, 8, N0), BF),
-            pltpu.VMEM((8, 2, 8, N1), BF),
-            pltpu.VMEM((8, 1, 8, N0), BF),
-            pltpu.VMEM((8, 1, 8, N1), BF),
-            pltpu.VMEM((8, 1, 8, PIX), BF),
-            pltpu.VMEM((8, 2, 8, N0), BF),
-            pltpu.VMEM((8, 2, 8, N1), BF),
-            pltpu.VMEM((8, 1, 8, N0), BF),
-            pltpu.VMEM((8, 1, 8, N1), BF),
-            pltpu.VMEM((8, 1, 8, PIX), BF),
+            pltpu.VMEM((3, 48, N0 + PIX), BF),
+            pltpu.VMEM((8, 8, 3 * N0 + PIX), BF),
+            pltpu.VMEM((8, 8, 3 * N1), BF),
+            pltpu.VMEM((8, 8, 3 * N0 + PIX), BF),
+            pltpu.VMEM((8, 8, 3 * N1), BF),
             dma((3,)), dma((2,)), dma((F,)),
             dma((F,)), dma((F,)), dma((F,)), dma((F,)),
             dma((F,)), dma((F,)), dma((F,)), dma((F,)),
-            dma((7, 3)), dma((7, 3)),
-            dma((5, 8)), dma((5, 8)),
+            dma((6, 3)), dma((6, 3)),
+            dma((2, 8)), dma((2, 8)),
         ],
         compiler_params=pltpu.CompilerParams(
             collective_id=0, has_side_effects=True, vmem_limit_bytes=56 << 20),
-    )(clip_groups, video_clips[0], conv_weight[0], norm_gain, cotangent[0])
+    )(clip_groups.reshape(1, 1), video_clips[0], conv_weight[0], norm_gain, cotangent[0])
     feat, dweight, dgain = pl.pallas_call(
         hand_over,
         out_shape=(

time: 67.7 us -> 66.9 us (0.988)
  Pallas kernels: 66.3 us -> 65.4 us
    pallas_call x1, Pallas kernels: 64.4 us -> 63.5 us  [body(): pl.pallas_call(kernel, out_shape=(jax.ShapeDtypeStruct((F, C, PIX), BF),...]
where the time goes in v4:
time: 66.9 us; the launch traced here: 66.7 us
  Pallas kernels  65.4 us (98%)
  between operations  1.29 us (2%)
    pallas_call x1, Pallas kernels, body(): pl.pallas_call(kernel, out_shape=(jax.ShapeDtypeStruct((F, C, PIX), BF),...  63.5 us
    pallas_call x1, Pallas kernels, body(): pl.pallas_call(hand_over, out_shape=(jax.ShapeDtypeStruct((F, C, PIX), BF...  1.9 us

profile of v4, /device:TPU:1, one launch (start us, length us, event | category | flops | bytes accessed | tf_op | source)
XLA Modules:
  0.0 66.7 jit_solution(6823869811391712078)
XLA Ops:
  1.3 63.5 %shard_map.76 = (bf16[9,192,128]{2,1,0:T(8,128)(2,1)}, f32[6,1,5184]{2,1,0:T(1,128)}, f32[1,128]{1,0:T(1,128)}) custom-call(s32[1,1]{1,0:T(1,128)} %bitcast.6.groups, bf16[9,192,128]{2,1,0:T(8,128)(2,1)} %bitcast.8, bf16[192,5184]{1,0:T(8,128)(2,1)} %bitcast.7, f32[1,192]{1,0:T(1,128)} %gain.1, bf16[9,192,128]{2,1,0:T(8,128)(2,1)} %bitcast.9), custom_call_target="tpu_custom_call" | custom-call | tf_op jit(solution)/shard_map/pallas_call | solution.py:483
  64.8 1.9 %shard_map.77 = (bf16[9,192,128]{2,1,0:T(8,128)(2,1)}, f32[6,1,5184]{2,1,0:T(1,128)}, f32[1,6]{1,0:T(1,128)}) custom-call(bf16[9,192,128]{2,1,0:T(8,128)(2,1)} %get-tuple-element.9.feat, f32[6,1,5184]{2,1,0:T(1,128)} %get-tuple-element.10.dweight, f32[1,128]{1,0:T(1,128)} %get-tuple-element.11.dgain), custom_call_target="tpu_custom_call" | custom-call | tf_op jit(solution)/shard_map/pallas_call | solution.py:536

commit v5 on v4

--- a/solution.py
+++ b/solution.py
@@ -48,8 +48,8 @@
     return patches
 
 
-def kernel(groups, video, weight_hbm, gain, cot, feat_hbm, dweight_hbm, dgain_hbm,
-           weight, feat, video_v, dweight, dgain, pre, xin, dyin, dysend, fac, scales, gain_b, gain_acc,
+def kernel(groups, video, weight_hbm, gain_hbm, cot, feat_hbm, dweight_hbm, dgain_hbm,
+           gain, weight, feat, video_v, dweight, dgain, pre, xin, dyin, dysend, fac, scales, gain_b, gain_acc,
            sp, xsp, dp_, wt, whalf, fold, dc, odc, acc0, acc1, col_sum,
            c0, c1, cg, d0, d1, dg, f0, f1, g0, g1,
            insem, outsem, featsem, fsend, frecv, bsend, brecv, psend, precv, csend, crecv,
@@ -68,22 +68,6 @@
             src_ref=src, dst_ref=dst, send_sem=ssem, recv_sem=rsem,
             device_id=where, device_id_type=pl.DeviceIdType.MESH)
 
-    early = pltpu.make_async_copy(weight_hbm.at[:, 2 * K3:], weight.at[:, 2 * K3:], insem.at[0])
-    late = pltpu.make_async_copy(weight_hbm.at[:, :2 * K3], weight.at[:, :2 * K3], insem.at[1])
-    clip = pltpu.make_async_copy(video, video_v, insem.at[2])
-    target = pltpu.make_async_copy(cot, dyin, insem.at[2])
-
-    @pl.when(seg == 0)
-    def _():
-        clip.start()
-
-    early.start()
-    late.start()
-
-    @pl.when(seg == 3)
-    def _():
-        target.start()
-
     barrier = pltpu.get_barrier_semaphore()
 
     def greet(where):
@@ -97,7 +81,25 @@
             greet(dev(lax.rem(zc + r, 4), xc, c))
             greet(dev(zc, lax.rem(xc + r, 4), c))
 
-    count = groups[...] * 4 - 3
+    early = pltpu.make_async_copy(weight_hbm.at[:, 2 * K3:], weight.at[:, 2 * K3:], insem.at[0])
+    late = pltpu.make_async_copy(weight_hbm.at[:, :2 * K3], weight.at[:, :2 * K3], insem.at[1])
+    clip = pltpu.make_async_copy(video, video_v, insem.at[2])
+    target = pltpu.make_async_copy(cot, dyin, insem.at[2])
+
+    @pl.when(seg == 0)
+    def _():
+        clip.start()
+
+    gains = pltpu.make_async_copy(gain_hbm, gain, insem.at[3])
+    gains.start()
+    early.start()
+    late.start()
+
+    @pl.when(seg == 3)
+    def _():
+        target.start()
+
+    count = groups[...].reshape(1, 1) * 4 - 3
 
     def keep(i):
         return jnp.where(i < count, 1.0, 0.0).astype(F32)
@@ -111,6 +113,7 @@
     dp_[0:K3, :] = zero_patch
     dp_[K3:2 * K3, :] = zero_patch
     pre[...] = jnp.zeros((C, PIX), F32)
+    gains.wait()
     gain_b[...] = jnp.broadcast_to(gain[...], (PIX, C)).T
     gain_acc[...] = jnp.zeros((C, PIX), F32)
     col_sum[...] = jnp.zeros((8, N0 + N1), F32)
@@ -190,8 +193,12 @@
         keep_copy(i).start()
         pair_copy(i).start()
         fac[i] = sig * (1.0 + conv * (1.0 - sig))
-        window = sp[pl.ds(pl.multiple_of((i + 1) * K3, 64), 2 * K3), :]
-        pre[...] = jnp.dot(weight[:, :2 * K3], window, preferred_element_type=F32)
+
+        @pl.when(i < F - 1)
+        def _():
+            window = sp[pl.ds(pl.multiple_of((i + 1) * K3, 64), 2 * K3), :]
+            pre[...] = jnp.dot(weight[:, :2 * K3], window, preferred_element_type=F32)
+
         return carry
 
     lax.fori_loop(0, F, forward, 0)
@@ -306,10 +313,13 @@
         dysend[i] = dx.astype(BF)
         bwd_copy(i).start()
         dconv_copy(i).start()
-        window = dp_[pl.ds(pl.multiple_of((n + 1) * K3, 64), 2 * K3), :]
-        pre[...] = jnp.dot(wt[:, :2 * K3], window, preferred_element_type=F32)
-
         gain_acc[...] += dnormed * x * scale
+
+        @pl.when(n < F - 1)
+        def _():
+            window = dp_[pl.ds(pl.multiple_of((n + 1) * K3, 64), 2 * K3), :]
+            pre[...] = jnp.dot(wt[:, :2 * K3], window, preferred_element_type=F32)
+
         return carry
 
     @pl.when(seg > 0)
@@ -470,10 +480,14 @@
         result.wait()
 
 
-def hand_over(feat, dweight, dgain, feat_out, dweight_out, dgain_out):
-    feat_out[...] = feat[...]
-    dweight_out[...] = dweight[...]
+def hand_over(feat, dweight, dgain, feat_out, dweight_out, dgain_out, sems):
+    copies = (pltpu.make_async_copy(feat, feat_out, sems.at[0]),
+              pltpu.make_async_copy(dweight, dweight_out, sems.at[1]))
+    for copy in copies:
+        copy.start()
     dgain_out[...] = dgain[:, 0:6]
+    for copy in copies:
+        copy.wait()
 
 
 def body(video_clips, conv_weight, norm_gain, cotangent, clip_groups):
@@ -487,9 +501,10 @@
             jax.ShapeDtypeStruct((6, 1, KK), F32),
             jax.ShapeDtypeStruct((1, 128), F32),
         ),
-        in_specs=[vmem, hbm, hbm, vmem, hbm],
+        in_specs=[vmem, hbm, hbm, hbm, hbm],
         out_specs=(hbm, hbm, hbm),
         scratch_shapes=[
+            pltpu.VMEM((1, C), F32),
             pltpu.VMEM((C, KK), BF),
             pltpu.VMEM((F, C, PIX), BF),
             pltpu.VMEM((F, C, PIX), BF),
@@ -524,15 +539,15 @@
             pltpu.VMEM((8, 8, 3 * N1), BF),
             pltpu.VMEM((8, 8, 3 * N0 + PIX), BF),
             pltpu.VMEM((8, 8, 3 * N1), BF),
-            dma((3,)), dma((2,)), dma((F,)),
+            dma((4,)), dma((2,)), dma((F,)),
             dma((F,)), dma((F,)), dma((F,)), dma((F,)),
             dma((F,)), dma((F,)), dma((F,)), dma((F,)),
             dma((6, 3)), dma((6, 3)),
             dma((2, 8)), dma((2, 8)),
         ],
         compiler_params=pltpu.CompilerParams(
-            collective_id=0, has_side_effects=True, vmem_limit_bytes=56 << 20),
-    )(clip_groups.reshape(1, 1), video_clips[0], conv_weight[0], norm_gain, cotangent[0])
+            collective_id=0, has_side_effects=True, vmem_limit_bytes=36 << 20),
+    )(clip_groups, *(pltpu.with_memory_space_constraint(v, pltpu.HBM) for v in (video_clips[0], conv_weight[0])), pltpu.with_memory_space_constraint(norm_gain, pltpu.HBM), pltpu.with_memory_space_constraint(cotangent[0], pltpu.HBM))
     feat, dweight, dgain = pl.pallas_call(
         hand_over,
         out_shape=(
@@ -540,8 +555,10 @@
             jax.ShapeDtypeStruct((6, 1, KK), F32),
             jax.ShapeDtypeStruct((1, 6), F32),
         ),
-        in_specs=[vmem, vmem, vmem],
-        out_specs=(vmem, vmem, vmem),
+        in_specs=[hbm, hbm, vmem],
+        out_specs=(hbm, hbm, vmem),
+        scratch_shapes=[dma((2,))],
+        compiler_params=pltpu.CompilerParams(vmem_limit_bytes=4 << 20),
     )(feat, dweight, dgain)
     return (feat[None, None], jnp.transpose(dweight, (1, 0, 2)), dgain)
 

time: 66.9 us -> 64.7 us (0.967)
  Pallas kernels: 65.4 us -> 63.2 us
    pallas_call x1, Pallas kernels: 63.5 us -> 61.9 us  [body(): pl.pallas_call(kernel, out_shape=(jax.ShapeDtypeStruct((F, C, PIX), BF),...]
where the time goes in v5:
time: 64.7 us; the launch traced here: 64.5 us
  Pallas kernels  63.2 us (98%)
  between operations  1.29 us (2%)
    pallas_call x1, Pallas kernels, body(): pl.pallas_call(kernel, out_shape=(jax.ShapeDtypeStruct((F, C, PIX), BF),...  61.9 us
    pallas_call x1, Pallas kernels, body(): pl.pallas_call(hand_over, out_shape=(jax.ShapeDtypeStruct((F, C, PIX), BF...  1.32 us

profile of v5, /device:TPU:1, one launch (start us, length us, event | category | flops | bytes accessed | tf_op | source)
XLA Modules:
  0.0 64.5 jit_solution(5441512384459262780)
XLA Ops:
  1.3 61.9 %shard_map.76 = (bf16[9,192,128]{2,1,0:T(8,128)(2,1)S(1)}, f32[6,1,5184]{2,1,0:T(1,128)S(1)}, f32[1,128]{1,0:T(1,128)S(1)}) custom-call(s32[1]{0:T(128)S(6)} %copy.8.groups, bf16[9,192,128]{2,1,0:T(8,128)(2,1)} %bitcast.6, bf16[192,5184]{1,0:T(8,128)(2,1)} %bitcast.5, f32[1,192]{1,0:T(1,128)} %gain_hbm.1, bf16[9,192,128]{2,1,0:T(8,128)(2,1)} %bitcast.7), custom_call_target="tpu_custom_call" | custom-call | tf_op jit(solution)/shard_map/pallas_call | solution.py:497
  63.2 1.3 %shard_map.77 = (bf16[9,192,128]{2,1,0:T(8,128)(2,1)}, f32[6,1,5184]{2,1,0:T(1,128)}, f32[1,6]{1,0:T(1,128)}) custom-call(bf16[9,192,128]{2,1,0:T(8,128)(2,1)S(1)} %get-tuple-element.9.feat, f32[6,1,5184]{2,1,0:T(1,128)S(1)} %get-tuple-element.10.dweight, f32[1,128]{1,0:T(1,128)S(1)} %get-tuple-element.11.dgain), custom_call_target="tpu_custom_call" | custom-call | tf_op jit(solution)/shard_map/pallas_call | solution.py:551

commit v6 on v5

--- a/solution.py
+++ b/solution.py
@@ -48,11 +48,11 @@
     return patches
 
 
-def kernel(groups, video, weight_hbm, gain_hbm, cot, feat_hbm, dweight_hbm, dgain_hbm,
-           gain, weight, feat, video_v, dweight, dgain, pre, xin, dyin, dysend, fac, scales, gain_b, gain_acc,
+def kernel(groups, video, weight_hbm, gain_hbm, cot, feat, dweight, dgain,
+           gain, weight, video_v, pre, xin, dyin, dysend, fac, scales, gain_b, gain_acc,
            sp, xsp, dp_, wt, whalf, fold, dc, odc, acc0, acc1, col_sum,
            c0, c1, cg, d0, d1, dg, f0, f1, g0, g1,
-           insem, outsem, featsem, fsend, frecv, bsend, brecv, psend, precv, csend, crecv,
+           insem, fsend, frecv, bsend, brecv, psend, precv, csend, crecv,
            s1send, s1recv, s2send, s2recv):
     seg = lax.axis_index("segment")
     d = lax.axis_index("dp")
@@ -147,6 +147,10 @@
     early.wait()
     late.wait()
 
+    @pl.when((seg == 0) & (core == 1))
+    def _():
+        own_weight()
+
     @pl.when(seg >= 2)
     def _():
         transpose_weight()
@@ -156,9 +160,6 @@
 
     def bwd_copy(i):
         return put(dysend.at[i], dyin.at[i], bsend.at[i], brecv.at[i], {"segment": lax.rem(seg + 3, 4)})
-
-    def keep_copy(i):
-        return pltpu.make_async_copy(feat.at[i], feat_hbm.at[i], featsem.at[i])
 
     def pair_copy(i):
         src = pl.multiple_of((i + 2) * K3 + HK * (1 - core), 32)
@@ -190,7 +191,6 @@
         def _():
             fwd_copy(i).start()
 
-        keep_copy(i).start()
         pair_copy(i).start()
         fac[i] = sig * (1.0 + conv * (1.0 - sig))
 
@@ -207,7 +207,7 @@
     def _():
         transpose_weight()
 
-    @pl.when(seg == 0)
+    @pl.when((seg == 0) & (core == 0))
     def _():
         own_weight()
 
@@ -334,8 +334,8 @@
         lax.fori_loop(0, F, arrived, 0)
         for t in range(3):
             frames = range(2 - t, F)
-            emit(t, 0, weight_product(t, frames, 0, N0))
-            emit(t, 1, weight_product(t, frames, N0, N1))
+            for h in ((1, 0) if t == 2 else (0, 1)):
+                emit(t, h, weight_product(t, frames, h * N0, N1 if h else N0))
 
     def take(n):
         i = F - 1 - n
@@ -357,17 +357,22 @@
                 accumulate(t, i)
             return carry
 
-        lax.fori_loop(1, F - 1, step, 0)
+        lax.fori_loop(1, F - 2, step, 0)
+        take(F - 2)
+        dconv_copy(2).wait_recv()
+        accumulate(0, 2)
         emit(0, 0, acc0[0])
         emit(0, 1, acc1[0])
+        accumulate(1, 2)
+        accumulate(2, 2)
+        add_columns(0)
         take(F - 1)
         dconv_copy(1).wait_recv()
         accumulate(1, 1)
         emit(1, 0, acc0[1])
         emit(1, 1, acc1[1])
         accumulate(2, 1)
-        for t in range(2):
-            add_columns(t)
+        add_columns(1)
         dconv_copy(0).wait_recv()
         accumulate(2, 0)
         emit(2, 1, acc1[2])
@@ -406,7 +411,6 @@
             collect(cg[me], dg[...], f0, 2 * N0, N0 + PIX)
 
     def settle(i, carry):
-        keep_copy(i).wait()
         pair_copy(i).wait_send()
         dconv_copy(i).wait_send()
 
@@ -466,18 +470,11 @@
     l8 = lax.broadcasted_iota(jnp.int32, (8, 128), 1)
     dgain[...] = jnp.sum(jnp.where(r8 == l8, gain_rows, 0.0), axis=0, keepdims=True)
 
-    results = (pltpu.make_async_copy(dweight, dweight_hbm, outsem.at[0]),
-               pltpu.make_async_copy(dgain, dgain_hbm, outsem.at[1]))
-    for result in results:
-        result.start()
-
     for h in range(2):
         for r in range(4):
             if r:
                 stage2_wait(h, r, core).wait_send()
             stage2_wait(h, r, 1 - core).wait_send()
-    for result in results:
-        result.wait()
 
 
 def hand_over(feat, dweight, dgain, feat_out, dweight_out, dgain_out, sems):
@@ -502,14 +499,11 @@
             jax.ShapeDtypeStruct((1, 128), F32),
         ),
         in_specs=[vmem, hbm, hbm, hbm, hbm],
-        out_specs=(hbm, hbm, hbm),
+        out_specs=(vmem, vmem, vmem),
         scratch_shapes=[
             pltpu.VMEM((1, C), F32),
             pltpu.VMEM((C, KK), BF),
             pltpu.VMEM((F, C, PIX), BF),
-            pltpu.VMEM((F, C, PIX), BF),
-            pltpu.VMEM((6, 1, KK), F32),
-            pltpu.VMEM((1, 128), F32),
             pltpu.VMEM((C, PIX), F32),
             pltpu.VMEM((F, C, PIX), BF),
             pltpu.VMEM((F, C, PIX), BF),
@@ -539,7 +533,7 @@
             pltpu.VMEM((8, 8, 3 * N1), BF),
             pltpu.VMEM((8, 8, 3 * N0 + PIX), BF),
             pltpu.VMEM((8, 8, 3 * N1), BF),
-            dma((4,)), dma((2,)), dma((F,)),
+            dma((4,)),
             dma((F,)), dma((F,)), dma((F,)), dma((F,)),
             dma((F,)), dma((F,)), dma((F,)), dma((F,)),
             dma((6, 3)), dma((6, 3)),

time: 64.7 us -> 63.8 us (0.986)
  Pallas kernels: 63.2 us -> 62.2 us
    pallas_call x1, Pallas kernels: 61.9 us -> 60.9 us  [body(): pl.pallas_call(kernel, out_shape=(jax.ShapeDtypeStruct((F, C, PIX), BF),...]
where the time goes in v6:
time: 63.8 us; the launch traced here: 63.7 us
  Pallas kernels  62.2 us (97%)
  between operations  1.45 us (2%)
    pallas_call x1, Pallas kernels, body(): pl.pallas_call(kernel, out_shape=(jax.ShapeDtypeStruct((F, C, PIX), BF),...  60.9 us
    pallas_call x1, Pallas kernels, body(): pl.pallas_call(hand_over, out_shape=(jax.ShapeDtypeStruct((F, C, PIX), BF...  1.32 us

profile of v6, /device:TPU:1, one launch (start us, length us, event | category | flops | bytes accessed | tf_op | source)
XLA Modules:
  0.0 63.7 jit_solution(14731062429470578709)
XLA Ops:
  1.3 60.9 %shard_map.76 = (bf16[9,192,128]{2,1,0:T(8,128)(2,1)S(1)}, f32[6,1,5184]{2,1,0:T(1,128)S(1)}, f32[1,128]{1,0:T(1,128)S(1)}) custom-call(s32[1]{0:T(128)S(6)} %copy.8.groups, bf16[9,192,128]{2,1,0:T(8,128)(2,1)} %bitcast.6, bf16[192,5184]{1,0:T(8,128)(2,1)} %bitcast.5, f32[1,192]{1,0:T(1,128)} %gain_hbm.1, bf16[9,192,128]{2,1,0:T(8,128)(2,1)} %bitcast.7), custom_call_target="tpu_custom_call" | custom-call | tf_op jit(solution)/shard_map/pallas_call | solution.py:494
  62.2 1.3 %shard_map.77 = (bf16[9,192,128]{2,1,0:T(8,128)(2,1)}, f32[6,1,5184]{2,1,0:T(1,128)}, f32[1,6]{1,0:T(1,128)}) custom-call(bf16[9,192,128]{2,1,0:T(8,128)(2,1)S(1)} %get-tuple-element.9.feat, f32[6,1,5184]{2,1,0:T(1,128)S(1)} %get-tuple-element.10.dweight, f32[1,128]{1,0:T(1,128)S(1)} %get-tuple-element.11.dgain), custom_call_target="tpu_custom_call" | custom-call | tf_op jit(solution)/shard_map/pallas_call | solution.py:545

commit v7 on v6

--- a/solution.py
+++ b/solution.py
@@ -240,14 +240,25 @@
         value = part.astype(BF)
         if t == 2 and h == 0:
             value = jnp.concatenate([value, gain_acc[...].astype(BF)], axis=1)
-        rows = jnp.dot(order(h), value, preferred_element_type=F32).astype(BF)
-        for q in range(4):
-            if h == 1:
-                c1[t, q] = rows[q * 48:(q + 1) * 48, :]
-            elif t < 2:
-                c0[t, q] = rows[q * 48:(q + 1) * 48, :]
-            else:
-                cg[q] = rows[q * 48:(q + 1) * 48, :]
+
+        def place(rows):
+            for q in range(4):
+                block = rows[q * 48:(q + 1) * 48, :]
+                if h == 1:
+                    c1[t, q] = block
+                elif t < 2:
+                    c0[t, q] = block
+                else:
+                    cg[q] = block
+
+        @pl.when(z_first(h) == 1)
+        def _():
+            place(value)
+
+        @pl.when(z_first(h) == 0)
+        def _():
+            place(jnp.dot(order(h), value, preferred_element_type=F32).astype(BF))
+
         for r in (2, 1, 3):
             stage1(t, h, r).start()
 

time: 63.8 us -> 63.8 us (level)
  no operation moved by 1% of the time
where the time goes in v7:
time: 63.8 us; the launch traced here: 63.6 us
  Pallas kernels  62.3 us (98%)
  between operations  1.29 us (2%)
    pallas_call x1, Pallas kernels, body(): pl.pallas_call(kernel, out_shape=(jax.ShapeDtypeStruct((F, C, PIX), BF),...  61 us
    pallas_call x1, Pallas kernels, body(): pl.pallas_call(hand_over, out_shape=(jax.ShapeDtypeStruct((F, C, PIX), BF...  1.32 us

profile of v7, /device:TPU:1, one launch (start us, length us, event | category | flops | bytes accessed | tf_op | source)
XLA Modules:
  0.0 63.6 jit_solution(16566199534023241747)
XLA Ops:
  1.3 61.0 %shard_map.76 = (bf16[9,192,128]{2,1,0:T(8,128)(2,1)S(1)}, f32[6,1,5184]{2,1,0:T(1,128)S(1)}, f32[1,128]{1,0:T(1,128)S(1)}) custom-call(s32[1]{0:T(128)S(6)} %copy.8.groups, bf16[9,192,128]{2,1,0:T(8,128)(2,1)} %bitcast.6, bf16[192,5184]{1,0:T(8,128)(2,1)} %bitcast.5, f32[1,192]{1,0:T(1,128)} %gain_hbm.1, bf16[9,192,128]{2,1,0:T(8,128)(2,1)} %bitcast.7), custom_call_target="tpu_custom_call" | custom-call | tf_op jit(solution)/shard_map/pallas_call | solution.py:505
  62.3 1.3 %shard_map.77 = (bf16[9,192,128]{2,1,0:T(8,128)(2,1)}, f32[6,1,5184]{2,1,0:T(1,128)}, f32[1,6]{1,0:T(1,128)}) custom-call(bf16[9,192,128]{2,1,0:T(8,128)(2,1)S(1)} %get-tuple-element.9.feat, f32[6,1,5184]{2,1,0:T(1,128)S(1)} %get-tuple-element.10.dweight, f32[1,128]{1,0:T(1,128)S(1)} %get-tuple-element.11.dgain), custom_call_target="tpu_custom_call" | custom-call | tf_op jit(solution)/shard_map/pallas_call | solution.py:556
